TPU v7x, 32 devices: a whole 2x2x4 slice. The times are simulated.
32 devices in a mesh: rows: 4 (over y, x), cols: 8 (over z, core).
Axes of the slice: x: 2, y: 2, z: 4, core: 2. Of those that a mesh axis runs over, the one named last changes fastest.
Arguments:
- object_tiles: float32 [2, 2, 3072, 6144], P(None, None, 'rows', 'cols'), may hold values from -6 to 6
- probe: float32 [2, 512, 512], replicated, may hold values from -6 to 6
- prop_phase: float32 [512, 512], replicated, may hold values from -3.140625 to 3.140625
- amplitudes: bfloat16 [4, 8, 1, 512, 512], P('rows', 'cols'), may hold values from 0 to 2
- offsets: int32 [4, 8, 1, 2], P('rows', 'cols'), may hold values from 0 to 512
- counts: int32 [4, 8], P('rows', 'cols'), may hold values from 0 to 1
- step_size: float32 [2], replicated, may hold values from 0.3 to 1
Outputs:
- updated: float32 [2, 2, 3072, 6144], P(None, None, 'rows', 'cols')
Inputs may be any that keep to these rules, and one draw needn't show every extreme that they name: `offsets`: row and column of a window's first cell in the device's tile extended by 128 cells on every side. `counts`: slots at or past a tile's count are ignored; a tile may have no probe position.
All inputs are finite; a program needn't handle non-finite values.
Results may differ from a plain program's by a relative error of at most 0.013.
The roundings to bfloat16 on the way count: a program that leaves them out, or rounds other values in their place, can miss the bound.
Values sent between devices are 32-bit elements; how exact they have to be, the bound alone decides.
A program may use at most 192 MiB of HBM per device.

v0:
```python
import math

import jax
import jax.numpy as jnp
from jax import lax
from jax.sharding import PartitionSpec as P

H = 128


def from_behind(block, axis, distance):
    devices = range(lax.axis_size(axis))
    route = [(i - distance, i) for i in devices if i - distance in devices]
    return lax.ppermute(block, axis, route)


def with_halo(block, sides, width):
    for axis, dim in sides:
        count = lax.axis_size(axis)
        forward = [(i, i + 1) for i in range(count - 1)]
        backward = [(target, source) for source, target in forward]
        low = lax.ppermute(
            lax.slice_in_dim(block, block.shape[dim] - width, None, axis=dim), axis, forward
        )
        high = lax.ppermute(lax.slice_in_dim(block, 0, width, axis=dim), axis, backward)
        block = jnp.concatenate([low, block, high], axis=dim)
    return block


def dft_tables(length, inverse):
    index = jnp.arange(length, dtype=jnp.int32)
    product = index[:, None] * index[None, :] % length
    angles = product.astype(jnp.float32) * (2.0 * math.pi / length)
    scaling = 1.0 / math.sqrt(length)
    direction = 1.0 if inverse else -1.0
    return (
        (jnp.cos(angles) * scaling).astype(jnp.bfloat16),
        (direction * jnp.sin(angles) * scaling).astype(jnp.bfloat16),
    )


def transform(real_part, imag_part, tables):
    table_re, table_im = tables
    left_re = real_part.astype(jnp.bfloat16)
    left_im = imag_part.astype(jnp.bfloat16)
    mid_re = jnp.dot(table_re, left_re, preferred_element_type=jnp.float32) - jnp.dot(
        table_im, left_im, preferred_element_type=jnp.float32
    )
    mid_im = jnp.dot(table_re, left_im, preferred_element_type=jnp.float32) + jnp.dot(
        table_im, left_re, preferred_element_type=jnp.float32
    )
    mid_re = mid_re.astype(jnp.bfloat16)
    mid_im = mid_im.astype(jnp.bfloat16)
    out_re = jnp.dot(mid_re, table_re, preferred_element_type=jnp.float32) - jnp.dot(
        mid_im, table_im, preferred_element_type=jnp.float32
    )
    out_im = jnp.dot(mid_re, table_im, preferred_element_type=jnp.float32) + jnp.dot(
        mid_im, table_re, preferred_element_type=jnp.float32
    )
    return (out_re, out_im)


def probe_gradient(window, probe, kernel_re, kernel_im, measured, forward, backward):
    first_re, first_im = (window[0, 0], window[0, 1])
    second_re, second_im = (window[1, 0], window[1, 1])
    probe_re, probe_im = (probe[0], probe[1])
    wave_re = probe_re * first_re - probe_im * first_im
    wave_im = probe_re * first_im + probe_im * first_re
    spec_re, spec_im = transform(wave_re, wave_im, forward)
    prop_re = spec_re * kernel_re - spec_im * kernel_im
    prop_im = spec_re * kernel_im + spec_im * kernel_re
    psi1_re, psi1_im = transform(prop_re, prop_im, backward)
    exit_re = psi1_re * second_re - psi1_im * second_im
    exit_im = psi1_re * second_im + psi1_im * second_re
    far_re, far_im = transform(exit_re, exit_im, forward)
    magnitude = jnp.sqrt(far_re * far_re + far_im * far_im + 1.0)
    factor = 1.0 - measured.astype(jnp.float32) / magnitude
    chi2_re, chi2_im = transform(far_re * factor, far_im * factor, backward)
    grad2_re = psi1_re * chi2_re + psi1_im * chi2_im
    grad2_im = psi1_re * chi2_im - psi1_im * chi2_re
    back_re = second_re * chi2_re + second_im * chi2_im
    back_im = second_re * chi2_im - second_im * chi2_re
    bspec_re, bspec_im = transform(back_re, back_im, forward)
    bprop_re = bspec_re * kernel_re + bspec_im * kernel_im
    bprop_im = bspec_im * kernel_re - bspec_re * kernel_im
    dwave_re, dwave_im = transform(bprop_re, bprop_im, backward)
    grad1_re = probe_re * dwave_re + probe_im * dwave_im
    grad1_im = probe_re * dwave_im - probe_im * dwave_re
    return jnp.stack([jnp.stack([grad1_re, grad1_im]), jnp.stack([grad2_re, grad2_im])])


def fold_cols(grad, margin):
    inner_width = grad.shape[3] - 2 * margin
    from_left = from_behind(grad[:, :, :, inner_width + margin :], "cols", 1)
    from_right = from_behind(grad[:, :, :, :margin], "cols", -1)
    inner = grad[:, :, :, margin : margin + inner_width]
    inner = inner.at[:, :, :, :margin].add(from_left)
    return inner.at[:, :, :, inner_width - margin :].add(from_right)


def fold_rows(grad, margin):
    inner_height = grad.shape[2] - 2 * margin
    from_above = from_behind(grad[:, :, inner_height + margin :, :], "rows", 1)
    from_below = from_behind(grad[:, :, :margin, :], "rows", -1)
    inner = grad[:, :, margin : margin + inner_height, :]
    inner = inner.at[:, :, :margin, :].add(from_above)
    return inner.at[:, :, inner_height - margin :, :].add(from_below)


def per_device(object_tiles, probe, prop_phase, amplitudes, offsets, counts, step_size):
    extended = with_halo(object_tiles, (("rows", 2), ("cols", 3)), H)
    width = probe.shape[1]
    forward = dft_tables(width, False)
    backward = dft_tables(width, True)
    kernel_re = jnp.cos(prop_phase)
    kernel_im = jnp.sin(prop_phase)
    zero = jnp.int32(0)
    blank = jnp.zeros(extended.shape, jnp.float32)
    weight = (0 < counts[0, 0]).astype(jnp.float32)
    corner = (zero, zero, offsets[0, 0, 0, 0], offsets[0, 0, 0, 1])
    window = lax.dynamic_slice(extended, corner, (2, 2, width, width))
    contribution = probe_gradient(
        window, probe, kernel_re, kernel_im, amplitudes[0, 0, 0], forward, backward
    )
    placed = lax.dynamic_update_slice(blank, weight * contribution, corner)
    grad = placed
    grad = fold_rows(fold_cols(grad, H), H)
    return object_tiles - step_size[:, None, None, None] * grad


def solution(mesh):
    return jax.shard_map(
        per_device,
        mesh=mesh,
        in_specs=(
            P(None, None, "rows", "cols"),
            P(),
            P(),
            P("rows", "cols", None, None, None),
            P("rows", "cols", None, None),
            P("rows", "cols"),
            P(),
        ),
        out_specs=P(None, None, "rows", "cols"),
        check_vma=False,
    )
```

profile of v0, /device:TPU:8, one launch (start us, length us, event | category | flops | bytes accessed | tf_op | source)
XLA Modules:
  0.0 507.1 jit_solution(10327728151282931783)
XLA Ops:
  7.4 32.2 %collective-permute-done = f32[2,2,128,768]{3,2,1,0:T(8,128)S(1)} collective-permute-done((f32[2,2,128,768]{3,2,1,0:T(8,128)S(1)}, f32[2,2,128,768]{3,2,1,0:T(8,128)S(1)}, u32[]{:S(2)}, u32[]{:S(2)}) %collective-permute-start) | collective-permute-done | bytes 1572896 | tf_op jit(solution)/shard_map/ppermute | solution.py:22
  45.1 30.2 %collective-permute-done.1 = f32[2,2,128,768]{3,2,1,0:T(8,128)S(1)} collective-permute-done((f32[2,2,128,768]{3,2,1,0:T(8,128)S(1)}, f32[2,2,128,768]{3,2,1,0:T(8,128)S(1)}, u32[]{:S(2)}, u32[]{:S(2)}) %collective-permute-start.1) | collective-permute-done | bytes 1572896 | tf_op jit(solution)/shard_map/ppermute | solution.py:25
  93.6 12.7 %collective-permute-done.3 = f32[2,2,1024,128]{3,2,1,0:T(8,128)} collective-permute-done((f32[2,2,1024,128]{3,2,1,0:T(8,128)}, f32[2,2,1024,128]{3,2,1,0:T(8,128)}, u32[]{:S(2)}, u32[]{:S(2)}) %collective-permute-start.3) | collective-permute-done | bytes 2097184 | tf_op jit(solution)/shard_map/ppermute | solution.py:25
  110.0 5.3 %fusion.1 = f32[2,2,512,512]{3,2,1,0:T(8,128)S(1)} fusion(s32[]{:T(128)S(6)} %select_n.112, s32[]{:T(128)S(6)} %select_n.113, f32[2,2,1024,128]{3,2,1,0:T(8,128)} %collective-permute-done.2, f32[2,2,1024,768]{3,2,1,0:T(8,128)} %constant_dynamic-update-slice_fusion, f32[2,2,1024,128]{3,2,1,0:T(8,128)} %collective-permute-done.3), kind=kLoop, calls=%fused_computation.5 | loop fusion | flops 2097152 | bytes 20971528 | tf_op jit(solution)/shard_map/concatenate | solution.py:26
  142.9 5.1 %convolution_subtract_fusion.10 = f32[512,512]{1,0:T(8,128)S(1)} fusion(f32[512,512]{1,0:T(8,128)S(1)} %fusion.50, bf16[512,512]{1,0:T(8,128)(2,1)S(1)} %fusion.7), kind=kOutput, calls=%fused_computation.41 | convolution fusion | flops 272891904 | bytes 2621440 | tf_op jit(solution)/shard_map/dot_general | solution.py:54
  148.0 5.4 %add_convert_fusion.3 = (bf16[512,512]{1,0:T(8,128)(2,1)S(1)}, bf16[512,512]{1,0:T(8,128)(2,1)S(1)}) fusion(f32[512,512]{1,0:T(8,128)S(1)} %get-tuple-element.79, f32[512,512]{1,0:T(8,128)S(1)} %convolution_subtract_fusion.10, f32[512,512]{1,0:T(8,128)S(1)} %get-tuple-element.80, f32[512,512]{1,0:T(8,128)S(1)} %fusion.54, bf16[512,512]{1,0:T(8,128)(2,1)S(1)} %fusion.7), kind=kOutput, calls=%fused_computation.91 | convolution fusion | flops 274989056 | bytes 5767168 | tf_op jit(solution)/shard_map/dot_general | solution.py:57
  180.3 5.1 %convolution_subtract_fusion.8 = f32[512,512]{1,0:T(8,128)S(1)} fusion(f32[512,512]{1,0:T(8,128)S(1)} %fusion.47, bf16[512,512]{1,0:T(8,128)(2,1)S(1)} %fusion.9), kind=kOutput, calls=%fused_computation.37 | convolution fusion | flops 272891904 | bytes 2621440 | tf_op jit(solution)/shard_map/dot_general | solution.py:54
  185.4 5.4 %add_convert_fusion.2 = (bf16[512,512]{1,0:T(8,128)(2,1)S(1)}, bf16[512,512]{1,0:T(8,128)(2,1)S(1)}, f32[512,512]{1,0:T(8,128)S(1)}) fusion(f32[512,512]{1,0:T(8,128)S(1)} %convolution_subtract_fusion.8, f32[2,2,512,512]{3,2,1,0:T(8,128)S(1)} %fusion.1, f32[512,512]{1,0:T(8,128)S(1)} %fusion.57, bf16[512,512]{1,0:T(8,128)(2,1)S(1)} %fusion.9), kind=kOutput, calls=%fused_computation.89 | convolution fusion | flops 274989056 | bytes 6815744 | tf_op jit(solution)/shard_map/dot_general | solution.py:57
  208.1 5.3 %fusion.44 = f32[512,512]{1,0:T(8,128)S(1)} fusion(bf16[512,512]{1,0:T(8,128)(2,1)S(1)} %fusion.10), kind=kOutput, calls=%fused_computation.110 | convolution fusion | flops 272629760 | bytes 1572864 | tf_op jit(solution)/shard_map/dot_general | solution.py:54
  217.9 5.1 %convolution_subtract_fusion.6 = f32[512,512]{1,0:T(8,128)S(1)} fusion(f32[512,512]{1,0:T(8,128)S(1)} %fusion.44, bf16[512,512]{1,0:T(8,128)(2,1)S(1)} %fusion.11), kind=kOutput, calls=%fused_computation.33 | convolution fusion | flops 272891904 | bytes 2621440 | tf_op jit(solution)/shard_map/dot_general | solution.py:54
  223.0 5.2 %multiply_convert_fusion = (bf16[512,512]{1,0:T(8,128)(2,1)S(1)}, bf16[512,512]{1,0:T(8,128)(2,1)S(1)}) fusion(f32[512,512]{1,0:T(8,128)S(1)} %convolution_subtract_fusion.6, bf16[1,1,1,512,512]{4,3,2,1,0:T(8,128)(2,1)S(1)} %copy-done.5, f32[512,512]{1,0:T(8,128)S(1)} %fusion.53, bf16[512,512]{1,0:T(8,128)(2,1)S(1)} %fusion.11), kind=kOutput, calls=%fused_computation.87 | convolution fusion | flops 275775488 | bytes 4194304 | tf_op jit(solution)/shard_map/dot_general | solution.py:57
  245.6 5.1 %fusion.41 = f32[512,512]{1,0:T(8,128)S(1)} fusion(bf16[512,512]{1,0:T(8,128)(2,1)S(1)} %fusion.12), kind=kOutput, calls=%fused_computation.107 | convolution fusion | flops 272629760 | bytes 1572864 | tf_op jit(solution)/shard_map/dot_general | solution.py:54
  260.3 5.5 %convolution_subtract_fusion.4 = f32[512,512]{1,0:T(8,128)S(1)} fusion(f32[512,512]{1,0:T(8,128)S(1)} %fusion.41, bf16[512,512]{1,0:T(8,128)(2,1)S(1)} %fusion.13), kind=kOutput, calls=%fused_computation.29 | convolution fusion | flops 272891904 | bytes 2621440 | tf_op jit(solution)/shard_map/dot_general | solution.py:54
  298.6 5.3 %subtract_convert_fusion = (bf16[512,512]{1,0:T(8,128)(2,1)S(1)}, bf16[512,512]{1,0:T(8,128)(2,1)S(1)}) fusion(f32[512,512]{1,0:T(8,128)S(1)} %get-tuple-element.80, f32[512,512]{1,0:T(8,128)S(1)} %convolution_add_fusion.2, f32[512,512]{1,0:T(8,128)S(1)} %get-tuple-element.79, f32[512,512]{1,0:T(8,128)S(1)} %fusion.38, bf16[512,512]{1,0:T(8,128)(2,1)S(1)} %fusion.15), kind=kOutput, calls=%fused_computation.83 | convolution fusion | flops 274989056 | bytes 5767168 | tf_op jit(solution)/shard_map/dot_general | solution.py:54
  321.2 5.3 %fusion.35 = f32[512,512]{1,0:T(8,128)S(1)} fusion(bf16[512,512]{1,0:T(8,128)(2,1)S(1)} %fusion.16), kind=kOutput, calls=%fused_computation.101 | convolution fusion | flops 272629760 | bytes 1572864 | tf_op jit(solution)/shard_map/dot_general | solution.py:54
  336.0 5.4 %fusion.27 = (f32[1,512,512]{2,1,0:T(8,128)S(1)}, f32[1,512,512]{2,1,0:T(8,128)S(1)}) fusion(f32[512,512]{1,0:T(8,128)S(1)} %convolution_add_fusion, f32[2,512,512]{2,1,0:T(8,128)S(1)} %copy-done.1, f32[512,512]{1,0:T(8,128)S(1)} %fusion.35, bf16[512,512]{1,0:T(8,128)(2,1)S(1)} %fusion.17), kind=kOutput, calls=%fused_computation.74 | convolution fusion | flops 274464768 | bytes 6815744 | tf_op jit(solution)/shard_map/dot_general | solution.py:54
  344.6 7.9 %broadcast_in_dim.2 = f32[2,2,1024,1024]{3,2,1,0:T(8,128)} broadcast(f32[]{:T(128)} %constant.128.clone.1), dimensions={} | broadcast | bytes 16777220 | tf_op jit(solution)/shard_map/broadcast_in_dim | solution.py:118
  352.5 29.0 %dynamic_update_slice.3 = f32[2,2,1024,1024]{3,2,1,0:T(8,128)} dynamic-update-slice(f32[2,2,1024,1024]{3,2,1,0:T(8,128)} %broadcast_in_dim.2, f32[2,2,512,512]{3,2,1,0:T(8,128)} %maximum_multiply_fusion, s32[]{:T(128)} %constant.130.clone.1, s32[]{:T(128)} %constant.130.clone.1, s32[]{:T(128)S(6)} %select_n.112, s32[]{:T(128)S(6)} %select_n.113) | dynamic-update-slice | bytes 8388612 | tf_op jit(solution)/shard_map/dynamic_update_slice | solution.py:125
  391.0 10.4 %slice.200 = f32[2,2,1024,768]{3,2,1,0:T(8,128)} slice(f32[2,2,1024,1024]{3,2,1,0:T(8,128)} %dynamic_update_slice.3), slice={[0:2], [0:2], [0:1024], [128:896]} | slice | bytes 25165824 | tf_op jit(solution)/shard_map/slice | solution.py:96
  401.5 11.4 %collective-permute-done.4 = f32[2,2,1024,128]{3,2,1,0:T(8,128)S(1)} collective-permute-done((f32[2,2,1024,128]{3,2,1,0:T(8,128)}, f32[2,2,1024,128]{3,2,1,0:T(8,128)S(1)}, u32[]{:S(2)}, u32[]{:S(2)}) %collective-permute-start.4) | collective-permute-done | bytes 2097184 | tf_op jit(solution)/shard_map/ppermute | solution.py:14
  426.5 8.0 %slice.205 = f32[2,2,768,768]{3,2,1,0:T(8,128)} slice(f32[2,2,1024,768]{3,2,1,0:T(8,128)} %fusion.2), slice={[0:2], [0:2], [128:896], [0:768]} | slice | bytes 18874368 | tf_op jit(solution)/shard_map/slice | solution.py:105
  434.6 23.7 %collective-permute-done.6 = f32[2,2,128,768]{3,2,1,0:T(8,128)S(1)} collective-permute-done((f32[2,2,128,768]{3,2,1,0:T(8,128)S(1)}, f32[2,2,128,768]{3,2,1,0:T(8,128)S(1)}, u32[]{:S(2)}, u32[]{:S(2)}) %collective-permute-start.6) | collective-permute-done | bytes 1572896 | tf_op jit(solution)/shard_map/ppermute | solution.py:14
  461.1 31.6 %collective-permute-done.7 = f32[2,2,128,768]{3,2,1,0:T(8,128)S(1)} collective-permute-done((f32[2,2,128,768]{3,2,1,0:T(8,128)S(1)}, f32[2,2,128,768]{3,2,1,0:T(8,128)S(1)}, u32[]{:S(2)}, u32[]{:S(2)}) %collective-permute-start.7) | collective-permute-done | bytes 1572896 | tf_op jit(solution)/shard_map/ppermute | solution.py:14
  495.6 11.4 %multiply_subtract_fusion = f32[2,2,768,768]{3,2,1,0:T(8,128)} fusion(f32[2,2,768,768]{3,2,1,0:T(8,128)} %param.15, f32[2,2,768,768]{3,2,1,0:T(8,128)} %fusion.4, f32[2]{0:T(128)S(1)} %copy-done.4), kind=kLoop, calls=%fused_computation.3 | loop fusion | flops 4718592 | bytes 28311560 | tf_op jit(solution)/shard_map/sub | solution.py:128
  (75 shorter events, 225.5 us)
Async XLA Ops:
  0.0 41.0 %copy-start = (f32[2,2,768,768]{3,2,1,0:T(8,128)S(1)}, f32[2,2,768,768]{3,2,1,0:T(8,128)}, u32[]{:S(2)}) copy-start(f32[2,2,768,768]{3,2,1,0:T(8,128)} %param.15) | copy-start | bytes 28311556
  2.4 37.3 %collective-permute-start = (f32[2,2,128,768]{3,2,1,0:T(8,128)S(1)}, f32[2,2,128,768]{3,2,1,0:T(8,128)S(1)}, u32[]{:S(2)}, u32[]{:S(2)}) collective-permute-start(f32[2,2,128,768]{3,2,1,0:T(8,128)S(1)} %get-tuple-element.60), channel_id=1, source_target_pairs={{0,8},{8,16},{16,24},{1,9},{9,17},{17,25},{2,10},{10,18},{18,26},{... | collective-permute-start | bytes 4718600 | tf_op jit(solution)/shard_map/ppermute | solution.py:22
  6.1 69.2 %collective-permute-start.1 = (f32[2,2,128,768]{3,2,1,0:T(8,128)S(1)}, f32[2,2,128,768]{3,2,1,0:T(8,128)S(1)}, u32[]{:S(2)}, u32[]{:S(2)}) collective-permute-start(f32[2,2,128,768]{3,2,1,0:T(8,128)S(1)} %get-tuple-element.59), channel_id=1, source_target_pairs={{8,0},{16,8},{24,16},{9,1},{17,9},{25,17},{10,2},{18,10},{26,18},{... | collective-permute-start | bytes 4718600 | tf_op jit(solution)/shard_map/ppermute | solution.py:25
  76.7 8.3 %copy-start.3 = (s32[1,1,1,2]{3,2,1,0:T(1,128)S(1)}, s32[1,1,1,2]{3,2,1,0:T(1,128)}, u32[]{:S(2)}) copy-start(s32[1,1,1,2]{3,2,1,0:T(1,128)} %param.19) | copy-start | bytes 28
  76.7 13.1 %copy-start.2 = (f32[512,512]{1,0:T(8,128)S(1)}, f32[512,512]{1,0:T(8,128)}, u32[]{:S(2)}) copy-start(f32[512,512]{1,0:T(8,128)} %param.17) | copy-start | bytes 3145732
  80.6 25.8 %collective-permute-start.3 = (f32[2,2,1024,128]{3,2,1,0:T(8,128)}, f32[2,2,1024,128]{3,2,1,0:T(8,128)}, u32[]{:S(2)}, u32[]{:S(2)}) collective-permute-start(f32[2,2,1024,128]{3,2,1,0:T(8,128)} %get-tuple-element.57), channel_id=1, source_target_pairs={{1,0},{2,1},{3,2},{4,3},{5,4},{6,5},{7,6},{9,8},{10,9},{11,10},{12... | collective-permute-start | bytes 6291464 | tf_op jit(solution)/shard_map/ppermute | solution.py:25
  82.5 27.5 %collective-permute-start.2 = (f32[2,2,1024,128]{3,2,1,0:T(8,128)S(1)}, f32[2,2,1024,128]{3,2,1,0:T(8,128)}, u32[]{:S(2)}, u32[]{:S(2)}) collective-permute-start(f32[2,2,1024,128]{3,2,1,0:T(8,128)S(1)} %get-tuple-element.58), channel_id=1, source_target_pairs={{0,1},{1,2},{2,3},{3,4},{4,5},{5,6},{6,7},{8,9},{9,10},{10,11},{11... | collective-permute-start | bytes 6291464 | tf_op jit(solution)/shard_map/ppermute | solution.py:22
  93.6 21.7 %copy-start.1 = (f32[2,512,512]{2,1,0:T(8,128)S(1)}, f32[2,512,512]{2,1,0:T(8,128)}, u32[]{:S(2)}) copy-start(f32[2,512,512]{2,1,0:T(8,128)} %param.16) | copy-start | bytes 6291460
  217.9 5.1 %copy-start.5 = (bf16[1,1,1,512,512]{4,3,2,1,0:T(8,128)(2,1)S(1)}, bf16[1,1,1,512,512]{4,3,2,1,0:T(8,128)(2,1)}, u32[]{:S(2)}) copy-start(bf16[1,1,1,512,512]{4,3,2,1,0:T(8,128)(2,1)} %param.18) | copy-start | bytes 1572868
  385.3 27.6 %collective-permute-start.4 = (f32[2,2,1024,128]{3,2,1,0:T(8,128)}, f32[2,2,1024,128]{3,2,1,0:T(8,128)S(1)}, u32[]{:S(2)}, u32[]{:S(2)}) collective-permute-start(f32[2,2,1024,128]{3,2,1,0:T(8,128)} %get-tuple-element.54), channel_id=1, source_target_pairs={{0,1},{1,2},{2,3},{3,4},{4,5},{5,6},{6,7},{8,9},{9,10},{10,11},{11... | collective-permute-start | bytes 6291464 | tf_op jit(solution)/shard_map/ppermute | solution.py:14
  387.2 29.1 %collective-permute-start.5 = (f32[2,2,1024,128]{3,2,1,0:T(8,128)S(1)}, f32[2,2,1024,128]{3,2,1,0:T(8,128)S(1)}, u32[]{:S(2)}, u32[]{:S(2)}) collective-permute-start(f32[2,2,1024,128]{3,2,1,0:T(8,128)S(1)} %get-tuple-element.53), channel_id=1, source_target_pairs={{1,0},{2,1},{3,2},{4,3},{5,4},{6,5},{7,6},{9,8},{10,9},{11,10},{12... | collective-permute-start | bytes 6291464 | tf_op jit(solution)/shard_map/ppermute | solution.py:14
  421.8 36.5 %collective-permute-start.6 = (f32[2,2,128,768]{3,2,1,0:T(8,128)S(1)}, f32[2,2,128,768]{3,2,1,0:T(8,128)S(1)}, u32[]{:S(2)}, u32[]{:S(2)}) collective-permute-start(f32[2,2,128,768]{3,2,1,0:T(8,128)S(1)} %get-tuple-element.56), channel_id=1, source_target_pairs={{0,8},{8,16},{16,24},{1,9},{9,17},{17,25},{2,10},{10,18},{18,26},{... | collective-permute-start | bytes 4718600 | tf_op jit(solution)/shard_map/ppermute | solution.py:14
  425.2 67.5 %collective-permute-start.7 = (f32[2,2,128,768]{3,2,1,0:T(8,128)S(1)}, f32[2,2,128,768]{3,2,1,0:T(8,128)S(1)}, u32[]{:S(2)}, u32[]{:S(2)}) collective-permute-start(f32[2,2,128,768]{3,2,1,0:T(8,128)S(1)} %get-tuple-element.55), channel_id=1, source_target_pairs={{8,0},{16,8},{24,16},{9,1},{17,9},{25,17},{10,2},{18,10},{26,18},{... | collective-permute-start | bytes 4718600 | tf_op jit(solution)/shard_map/ppermute | solution.py:14
  434.6 61.0 %copy-start.4 = (f32[2]{0:T(128)S(1)}, f32[2]{0:T(128)}, u32[]{:S(2)}) copy-start(f32[2]{0:T(128)} %param.21) | copy-start | bytes 28
where the time goes:
time: 512 us; the launch traced here: 507 us
  matrix products  224 us (44%)
  waiting for transfers between devices  145 us (28%)
  local copies, waits for them, and re-layouts  78.9 us (15%)
  other arithmetic  33.8 us (7%)
  starting transfers between devices  19.8 us (4%)
    ppermute x4, waiting for transfers between devices, from_behind(): return lax.ppermute(block, axis, route)  66.7 us
    ppermute x2, waiting for transfers between devices, with_halo(): lax.ppermute(lax.slice_in_dim(block, 0, width, axis=dim), axis, backward)  42.9 us
    ppermute x2, waiting for transfers between devices, with_halo(): lax.ppermute(lax.slice_in_dim(block, block.shape[dim] - width, None, axis...  35.8 us
    dot_general x6, matrix products, transform(): jnp.dot(mid_im, table_im, preferred_element_type=jnp.float32)  31.4 us
    dot_general x6, matrix products, transform(): jnp.dot(mid_im, table_re, preferred_element_type=jnp.float32)  31.2 us
    dot_general x6, matrix products, transform(): jnp.dot(mid_re, table_re, preferred_element_type=jnp.float32)  30.3 us
    dot_general x6, matrix products, transform(): jnp.dot(mid_re, table_im, preferred_element_type=jnp.float32)  29.5 us
    dynamic_update_slice x1, local copies, waits for them, and re-layouts, per_device(): placed = lax.dynamic_update_slice(blank, weight * contribution, corner)  29 us
  transfers between devices with their start and end apart: 8, of which 7 were waited for; matrix products, arithmetic and copies ran while one was open for 7% of the time, Pallas kernels for 0%

commit v1 on v0

v1 whole, which is shorter than its diff:
```python
import functools
import math

import jax
import jax.numpy as jnp
import numpy as np
from jax import lax
from jax.experimental import pallas as pl
from jax.experimental.pallas import tpu as pltpu
from jax.sharding import PartitionSpec as P

H = 128
LANES = 128
SUBLANES = 8
ROWS = 256
F32 = jnp.float32
BF16 = jnp.bfloat16


def shifted(block, axis, step):
    count = lax.axis_size(axis)
    route = [(i, i + step) for i in range(count) if 0 <= i + step < count]
    return lax.ppermute(block, axis, route)


def dft_table(length):
    index = np.arange(length, dtype=np.int64)
    angles = ((index[:, None] * index[None, :]) % length).astype(np.float32) * np.float32(
        2.0 * math.pi / length
    )
    scaling = np.float32(1.0 / math.sqrt(length))
    return (
        jnp.asarray((np.cos(angles) * scaling).astype(BF16)),
        jnp.asarray((-np.sin(angles) * scaling).astype(BF16)),
    )


def params(flops=0, moved=0, mib=48):
    return dict(
        compiler_params=pltpu.CompilerParams(vmem_limit_bytes=mib << 20),
        cost_estimate=pl.CostEstimate(flops=flops, bytes_accessed=moved, transcendentals=0),
    )


SMEM = pl.BlockSpec(memory_space=pltpu.SMEM)
VMEM = pl.BlockSpec(memory_space=pltpu.VMEM)


def take_columns(wide, start, width):
    base = pl.multiple_of(start // LANES * LANES, LANES)
    piece = wide[:, pl.ds(base, width + LANES)]
    return pltpu.roll(piece, (width + LANES) - start % LANES, axis=1)[:, :width]


def edges_kernel(cols_ref, top, bottom, lt, lb, rt, rb, up, down, wide):
    inner = top.shape[-1]
    width = up.shape[-1]
    for left, tile, right, out, which in ((lt, top, rt, up, 1), (lb, bottom, rb, down, 2)):
        wide[:, :H] = left[0]
        wide[:, H : H + inner] = tile[0, 0]
        wide[:, H + inner : 2 * H + inner] = right[0]
        wide[:, 2 * H + inner :] = jnp.zeros((wide.shape[0], LANES), F32)
        out[0] = take_columns(wide, cols_ref[which], width)


def edges(cols, tile, left, right, s, width):
    rows, inner = tile.shape[2:]
    last = rows // H - 1
    side = lambda r: pl.BlockSpec((1, H, H), lambda c: (c, r, 0))
    return pl.pallas_call(
        edges_kernel,
        grid=(2,),
        in_specs=[
            SMEM,
            pl.BlockSpec((1, 1, H, inner), lambda c: (s, c, 0, 0)),
            pl.BlockSpec((1, 1, H, inner), lambda c: (s, c, last, 0)),
            side(0),
            side(last),
            side(0),
            side(last),
        ],
        out_specs=[pl.BlockSpec((1, H, width), lambda c: (c, 0, 0))] * 2,
        out_shape=[jax.ShapeDtypeStruct((2, H, width), F32)] * 2,
        scratch_shapes=[pltpu.VMEM((H, inner + 2 * H + LANES), F32)],
        name=f"edges{s}",
        **params(0, 3 << 20),
    )(cols, tile, tile, left, left, right, right)


def middle_kernel(cols_ref, tile, left, right, out, wide):
    inner = tile.shape[-1]
    wide[:, :H] = left[0]
    wide[:, H : H + inner] = tile[0, 0]
    wide[:, H + inner : 2 * H + inner] = right[0]
    wide[:, 2 * H + inner :] = jnp.zeros((wide.shape[0], LANES), F32)
    out[0] = take_columns(wide, cols_ref[0], out.shape[-1])


def middle(cols, tile, left, right, s, width):
    rows, inner = tile.shape[2:]
    return pl.pallas_call(
        middle_kernel,
        grid=(2, rows // H),
        in_specs=[
            SMEM,
            pl.BlockSpec((1, 1, H, inner), lambda c, r: (s, c, r, 0)),
            pl.BlockSpec((1, H, H), lambda c, r: (c, r, 0)),
            pl.BlockSpec((1, H, H), lambda c, r: (c, r, 0)),
        ],
        out_specs=pl.BlockSpec((1, H, width), lambda c, r: (c, r, 0)),
        out_shape=jax.ShapeDtypeStruct((2, rows, width), F32),
        scratch_shapes=[pltpu.VMEM((H, inner + 2 * H + LANES), F32)],
        name=f"middle{s}",
        **params(0, 9 << 20),
    )(cols, tile, left, right)


def make_tables(cos_ref, sin_ref, fwd, bwd):
    n = cos_ref.shape[0]
    c, s = cos_ref[...], sin_ref[...]
    for table, sine in ((fwd, s), (bwd, -s)):
        table[:n, :n] = c
        table[n:, n:] = c
        table[n:, :n] = sine
        table[:n, n:] = -sine


def transform(src, left, right, mid, epilogue):
    n = mid.shape[0]

    @pl.loop(0, n // ROWS)
    def _(i):
        at = pl.ds(pl.multiple_of(i * ROWS, ROWS), ROWS)
        low = pl.ds(pl.multiple_of(n + i * ROWS, ROWS), ROWS)
        mid[at, :n] = jnp.dot(left[at, :], src[...], preferred_element_type=F32).astype(BF16)
        mid[at, n:] = jnp.dot(left[low, :], src[...], preferred_element_type=F32).astype(BF16)

    @pl.loop(0, n // ROWS)
    def _(i):
        at = pl.ds(pl.multiple_of(i * ROWS, ROWS), ROWS)
        low = pl.ds(pl.multiple_of(n + i * ROWS, ROWS), ROWS)
        out = jnp.dot(mid[at, :], right[...], preferred_element_type=F32)
        epilogue(i, at, low, out[:, :n], out[:, n:])


def take_rows(field, part, start, offset, height):
    base = pl.multiple_of(start // SUBLANES * SUBLANES + offset, SUBLANES)
    piece = field[part, pl.ds(base, height + SUBLANES), :]
    return pltpu.roll(piece, (height + SUBLANES) - start % SUBLANES, axis=0)[:height]


def add_rows(field, part, start, offset, block):
    height = block.shape[0]
    base = pl.multiple_of(start // SUBLANES * SUBLANES + offset, SUBLANES)
    block = jnp.concatenate([block, jnp.zeros((SUBLANES, block.shape[1]), F32)], axis=0)
    field[part, pl.ds(base, height + SUBLANES), :] += pltpu.roll(block, start % SUBLANES, axis=0)


def load_window(top, body, bottom, window):
    rows = body.shape[1]
    window[:, :H] = top[...]
    window[:, H : H + rows] = body[...]
    window[:, H + rows : 2 * H + rows] = bottom[...]


def first_kernel(rows_ref, top, body, bottom, probe, k, cos, sin, psi, window, fwd, bwd, src, mid):
    n = cos.shape[0]
    make_tables(cos, sin, fwd, bwd)
    load_window(top, body, bottom, window)
    start = rows_ref[0]

    @pl.loop(0, n // H)
    def _(i):
        at = pl.ds(pl.multiple_of(i * H, H), H)
        low = pl.ds(pl.multiple_of(n + i * H, H), H)
        a_re = take_rows(window, 0, start, i * H, H)
        a_im = take_rows(window, 1, start, i * H, H)
        q_re, q_im = probe[0, at, :], probe[1, at, :]
        src[at, :] = (q_re * a_re - q_im * a_im).astype(BF16)
        src[low, :] = (q_re * a_im + q_im * a_re).astype(BF16)

    def propagate(i, at, low, re, im):
        k_re, k_im = k[0, at, :], k[1, at, :]
        src[at, :] = (re * k_re - im * k_im).astype(BF16)
        src[low, :] = (re * k_im + im * k_re).astype(BF16)

    def keep(i, at, low, re, im):
        psi[0, at, :] = re
        psi[1, at, :] = im

    transform(src, fwd, bwd, mid, propagate)
    transform(src, bwd, fwd, mid, keep)


def second_kernel(
    rows_ref, count_ref, top, body, bottom, psi, amp, cos, sin, grad, back, window, fwd, bwd, src, mid
):
    n = cos.shape[0]
    make_tables(cos, sin, fwd, bwd)
    load_window(top, body, bottom, window)
    start = rows_ref[0]
    weight = jnp.where(count_ref[0] > 0, 1.0, 0.0).astype(F32)
    grad[...] = jnp.zeros_like(grad)

    @pl.loop(0, n // H)
    def _(i):
        at = pl.ds(pl.multiple_of(i * H, H), H)
        low = pl.ds(pl.multiple_of(n + i * H, H), H)
        b_re = take_rows(window, 0, start, i * H, H)
        b_im = take_rows(window, 1, start, i * H, H)
        p_re, p_im = psi[0, at, :], psi[1, at, :]
        src[at, :] = (p_re * b_re - p_im * b_im).astype(BF16)
        src[low, :] = (p_re * b_im + p_im * b_re).astype(BF16)

    def detect(i, at, low, re, im):
        factor = 1.0 - amp[at, :].astype(F32) / jnp.sqrt(re * re + im * im + 1.0)
        src[at, :] = (re * factor).astype(BF16)
        src[low, :] = (im * factor).astype(BF16)

    def spread(i, at, low, re, im):
        p_re, p_im = psi[0, at, :], psi[1, at, :]
        b_re = take_rows(window, 0, start, i * ROWS, ROWS)
        b_im = take_rows(window, 1, start, i * ROWS, ROWS)
        add_rows(grad, 0, start, i * ROWS, weight * (p_re * re + p_im * im))
        add_rows(grad, 1, start, i * ROWS, weight * (p_re * im - p_im * re))
        back[at, :] = (b_re * re + b_im * im).astype(BF16)
        back[low, :] = (b_re * im - b_im * re).astype(BF16)

    transform(src, fwd, bwd, mid, detect)
    transform(src, bwd, fwd, mid, spread)


def third_kernel(rows_ref, count_ref, back, probe, k, cos, sin, grad, fwd, bwd, src, mid):
    make_tables(cos, sin, fwd, bwd)
    start = rows_ref[0]
    weight = jnp.where(count_ref[0] > 0, 1.0, 0.0).astype(F32)
    grad[...] = jnp.zeros_like(grad)

    def propagate(i, at, low, re, im):
        k_re, k_im = k[0, at, :], k[1, at, :]
        src[at, :] = (re * k_re + im * k_im).astype(BF16)
        src[low, :] = (im * k_re - re * k_im).astype(BF16)

    def finish(i, at, low, re, im):
        q_re, q_im = probe[0, at, :], probe[1, at, :]
        add_rows(grad, 0, start, i * ROWS, weight * (q_re * re + q_im * im))
        add_rows(grad, 1, start, i * ROWS, weight * (q_re * im - q_im * re))

    transform(back, fwd, bwd, mid, propagate)
    transform(src, bwd, fwd, mid, finish)


def work(n):
    return [
        pltpu.VMEM((2 * n, 2 * n), BF16),
        pltpu.VMEM((2 * n, 2 * n), BF16),
        pltpu.VMEM((2 * n, n), BF16),
        pltpu.VMEM((n, 2 * n), BF16),
    ]


def place_kernel(s, cols_ref, step_ref, grad, above, below, tile, *rest):
    out, to_left, to_right, wide = rest[-4:]
    rows, inner = tile.shape[2:]
    width = grad.shape[-1]
    wide[...] = jnp.zeros_like(wide)

    def add(row, block, start):
        base = pl.multiple_of(start // LANES * LANES, LANES)
        block = jnp.concatenate([block, jnp.zeros((H, LANES), F32)], axis=1)
        wide[pl.ds(row, H), pl.ds(base, width + LANES)] += pltpu.roll(block, start % LANES, axis=1)

    @pl.loop(0, rows // H)
    def _(i):
        add(pl.multiple_of(i * H, H), grad[0, pl.ds(pl.multiple_of(H + i * H, H), H), :], cols_ref[0])

    add(0, above[0], cols_ref[1])
    add(rows - H, below[0], cols_ref[2])
    out[0, 0] = tile[0, 0] - step_ref[s] * wide[:, H : H + inner]
    to_left[0] = wide[:, :H]
    to_right[0] = wide[:, H + inner : 2 * H + inner]


def place(cols, step, grad, above, below, tile, s, so_far):
    rows, inner = tile.shape[2:]
    width = grad.shape[-1]
    plane = pl.BlockSpec((1, 1, rows, inner), lambda c: (s, c, 0, 0))
    edge = pl.BlockSpec((1, H, width), lambda c: (c, 0, 0))
    side = pl.BlockSpec((1, rows, H), lambda c: (c, 0, 0))
    more = [] if so_far is None else [so_far]
    return pl.pallas_call(
        functools.partial(place_kernel, s),
        grid=(2,),
        in_specs=[SMEM, SMEM, pl.BlockSpec((1,) + grad.shape[1:], lambda c: (c, 0, 0)), edge, edge, plane]
        + [pl.BlockSpec(memory_space=pl.ANY)] * len(more),
        out_specs=[plane, side, side],
        out_shape=[
            jax.ShapeDtypeStruct(tile.shape, F32),
            jax.ShapeDtypeStruct((2, rows, H), F32),
            jax.ShapeDtypeStruct((2, rows, H), F32),
        ],
        scratch_shapes=[pltpu.VMEM((rows, inner + 2 * H + LANES), F32)],
        input_output_aliases={6: 0} if more else {},
        name=f"place{s}",
        **params(0, 14 << 20),
    )(cols, step, grad, above, below, tile, *more)


def border_kernel(s, step_ref, left, right, old, out):
    @pl.when(pl.program_id(1) == 0)
    def _():
        out[0, 0] = old[0, 0] - step_ref[s] * left[0]

    @pl.when(pl.program_id(1) == 1)
    def _():
        out[0, 0] = old[0, 0] - step_ref[s] * right[0]


def border(step, left, right, out, s):
    rows, inner = out.shape[2:]
    far = inner // H - 1
    strip = pl.BlockSpec((1, 1, rows, H), lambda c, e: (s, c, 0, e * far))
    side = pl.BlockSpec((1, rows, H), lambda c, e: (c, 0, 0))
    return pl.pallas_call(
        functools.partial(border_kernel, s),
        grid=(2, 2),
        in_specs=[SMEM, side, side, strip],
        out_specs=strip,
        out_shape=jax.ShapeDtypeStruct(out.shape, F32),
        input_output_aliases={3: 0},
        name=f"border{s}",
        **params(0, 5 << 20),
    )(step, left, right, out)


def per_device(object_tiles, probe, prop_phase, amplitudes, offsets, counts, step_size):
    n = probe.shape[1]
    rows, inner = object_tiles.shape[2:]
    cos, sin = dft_table(n)
    kernel = jnp.stack([jnp.cos(prop_phase), jnp.sin(prop_phase)])
    mine = offsets[0, 0, 0]
    above = shifted(mine, "rows", 1)
    below = shifted(mine, "rows", -1)
    cols = jnp.stack([mine[1], above[1], below[1]])
    row = mine[:1]
    count = counts[0]

    lefts, rights, tops, bottoms, bodies = [], [], [], [], []
    for s in range(2):
        lefts.append(shifted(object_tiles[s, :, :, inner - H :], "cols", 1))
        rights.append(shifted(object_tiles[s, :, :, :H], "cols", -1))
    for s in range(2):
        up, down = edges(cols, object_tiles, lefts[s], rights[s], s, n)
        tops.append(shifted(down, "rows", 1))
        bottoms.append(shifted(up, "rows", -1))
    for s in range(2):
        bodies.append(middle(cols, object_tiles, lefts[s], rights[s], s, n))

    per_transform = 2 * 2 * (2 * n) * (2 * n) * n
    ext = jax.ShapeDtypeStruct((2, rows + 2 * H + SUBLANES, n), F32)
    field = jax.ShapeDtypeStruct((2, n, n), F32)
    window = pltpu.VMEM(ext.shape, F32)
    psi = pl.pallas_call(
        first_kernel,
        in_specs=[SMEM] + [VMEM] * 7,
        out_specs=VMEM,
        out_shape=field,
        scratch_shapes=[window] + work(n),
        name="first",
        **params(2 * per_transform, 12 << 20),
    )(row, tops[0], bodies[0], bottoms[0], probe, kernel, cos, sin)
    grad2, back = pl.pallas_call(
        second_kernel,
        in_specs=[SMEM] * 2 + [VMEM] * 7,
        out_specs=[VMEM, VMEM],
        out_shape=[ext, jax.ShapeDtypeStruct((2 * n, n), BF16)],
        scratch_shapes=[window] + work(n),
        name="second",
        **params(2 * per_transform, 14 << 20),
    )(row, count, tops[1], bodies[1], bottoms[1], psi, amplitudes[0, 0, 0], cos, sin)
    grad1 = pl.pallas_call(
        third_kernel,
        in_specs=[SMEM] * 2 + [VMEM] * 5,
        out_specs=VMEM,
        out_shape=ext,
        scratch_shapes=work(n),
        name="third",
        **params(2 * per_transform, 12 << 20),
    )(row, count, back, probe, kernel, cos, sin)

    out = None
    sides = []
    for s, grad in ((1, grad2), (0, grad1)):
        from_above = shifted(grad[:, rows + H : rows + 2 * H], "rows", 1)
        from_below = shifted(grad[:, :H], "rows", -1)
        out, to_left, to_right = place(
            cols, step_size, grad, from_above, from_below, object_tiles, s, out
        )
        sides.append((s, shifted(to_right, "cols", 1), shifted(to_left, "cols", -1)))
    for s, left, right in sides:
        out = border(step_size, left, right, out, s)
    return out


def solution(mesh):
    return jax.shard_map(
        per_device,
        mesh=mesh,
        in_specs=(
            P(None, None, "rows", "cols"),
            P(),
            P(),
            P("rows", "cols", None, None, None),
            P("rows", "cols", None, None),
            P("rows", "cols"),
            P(),
        ),
        out_specs=P(None, None, "rows", "cols"),
        check_vma=False,
    )
```

time: 512 us -> 173 us (0.34)
  the two profiles are of different devices: /device:TPU:8 before, /device:TPU:15 now
where the time goes in v1:
time: 173 us; the launch traced here: 172 us
  Pallas kernels  81.9 us (47%)
  starting transfers between devices  55.1 us (32%)
  waiting for transfers between devices  16.8 us (10%)
  local copies, waits for them, and re-layouts  13.6 us (8%)
  other arithmetic  3.61 us (2%)
    ppermute x18, starting transfers between devices, shifted(): return lax.ppermute(block, axis, route)  55.1 us
    ppermute x18, waiting for transfers between devices, shifted(): return lax.ppermute(block, axis, route)  16.8 us
    pallas_call x2, Pallas kernels, place(): pl.pallas_call(functools.partial(place_kernel, s), grid=(2,), in_specs=[S...  16.5 us
    pallas_call x2, Pallas kernels, middle(): pl.pallas_call(middle_kernel, grid=(2, rows // H), in_specs=[SMEM, pl.Blo...  15.6 us
    pallas_call x1, Pallas kernels, per_device(): pl.pallas_call(second_kernel, in_specs=[SMEM] * 2 + [VMEM] * 7, out_specs...  15.1 us
    pallas_call x1, Pallas kernels, per_device(): pl.pallas_call(third_kernel, in_specs=[SMEM] * 2 + [VMEM] * 5, out_specs=...  12.1 us
    pallas_call x1, Pallas kernels, per_device(): pl.pallas_call(first_kernel, in_specs=[SMEM] + [VMEM] * 7, out_specs=VMEM...  11.5 us
    pallas_call x2, Pallas kernels, border(): pl.pallas_call(functools.partial(border_kernel, s), grid=(2, 2), in_specs...  7.38 us
  transfers between devices with their start and end apart: 18, of which 6 were waited for; matrix products, arithmetic and copies ran while one was open for 6% of the time, Pallas kernels for 37%

profile of v1, /device:TPU:15, one launch (start us, length us, event | category | flops | bytes accessed | tf_op | source)
XLA Modules:
  0.0 172.0 jit_solution(959072925054876255)
XLA Ops:
  2.1 2.6 %collective-permute-start.7 = (f32[2,768,128]{2,1,0:T(8,128)S(1)}, f32[2,768,128]{2,1,0:T(8,128)S(1)}, u32[]{:S(2)}, u32[]{:S(2)}) collective-permute-start(f32[2,768,128]{2,1,0:T(8,128)S(1)} %get-tuple-element.29), channel_id=1, source_target_pairs={{1,0},{2,1},{3,2},{4,3},{5,4},{6,5},{7,6},{9,8},{10,9},{11,10},{12... | collective-permute-start | bytes 2359304 | tf_op jit(solution)/shard_map/ppermute | solution.py:23
  4.7 3.1 %collective-permute-start.6 = (f32[2,768,128]{2,1,0:T(8,128)S(1)}, f32[2,768,128]{2,1,0:T(8,128)S(1)}, u32[]{:S(2)}, u32[]{:S(2)}) collective-permute-start(f32[2,768,128]{2,1,0:T(8,128)S(1)} %get-tuple-element.30), channel_id=1, source_target_pairs={{0,1},{1,2},{2,3},{3,4},{4,5},{5,6},{6,7},{8,9},{9,10},{10,11},{11... | collective-permute-start | bytes 2359304 | tf_op jit(solution)/shard_map/ppermute | solution.py:23
  9.8 3.6 %collective-permute-start.2 = (f32[2,768,128]{2,1,0:T(8,128)S(1)}, f32[2,768,128]{2,1,0:T(8,128)S(1)}, u32[]{:S(2)}, u32[]{:S(2)}) collective-permute-start(f32[2,768,128]{2,1,0:T(8,128)S(1)} %get-tuple-element.32), channel_id=1, source_target_pairs={{0,1},{1,2},{2,3},{3,4},{4,5},{5,6},{6,7},{8,9},{9,10},{10,11},{11... | collective-permute-start | bytes 2359304 | tf_op jit(solution)/shard_map/ppermute | solution.py:23
  13.4 2.2 %collective-permute-start.1 = (s32[2]{0:T(128)S(1)}, s32[2]{0:T(128)S(1)}, u32[]{:S(2)}, u32[]{:S(2)}) collective-permute-start(s32[2]{0:T(128)S(1)} %bitcast.20), channel_id=1, source_target_pairs={{8,0},{16,8},{24,16},{9,1},{17,9},{25,17},{10,2},{18,10},{26,18},{... | collective-permute-start | bytes 32 | tf_op jit(solution)/shard_map/ppermute | solution.py:23
  18.2 3.3 %collective-permute-done = s32[2]{0:T(128)S(1)} collective-permute-done((s32[2]{0:T(128)S(1)}, s32[2]{0:T(128)S(1)}, u32[]{:S(2)}, u32[]{:S(2)}) %collective-permute-start) | collective-permute-done | bytes 40 | tf_op jit(solution)/shard_map/ppermute | solution.py:23
  27.3 4.6 %collective-permute-start.9 = (f32[2,128,512]{2,1,0:T(8,128)S(1)}, f32[2,128,512]{2,1,0:T(8,128)S(1)}, u32[]{:S(2)}, u32[]{:S(2)}) collective-permute-start(f32[2,128,512]{2,1,0:T(8,128)S(1)} %get-tuple-element.20), channel_id=1, source_target_pairs={{8,0},{16,8},{24,16},{9,1},{17,9},{25,17},{10,2},{18,10},{26,18},{... | collective-permute-start | bytes 1572872 | tf_op jit(solution)/shard_map/ppermute | solution.py:23
  32.6 3.7 %cosine_bitcast_fusion = (f32[1,512,512]{2,1,0:T(8,128)S(1)}, f32[1,512,512]{2,1,0:T(8,128)S(1)}) fusion(f32[512,512]{1,0:T(8,128)S(1)} %copy-done.7), kind=kLoop, calls=%fused_computation.2 | loop fusion | bytes 3145728 | tf_op jit(solution)/shard_map/stack | solution.py:340
  39.5 4.9 %collective-permute-start.5 = (f32[2,128,512]{2,1,0:T(8,128)S(1)}, f32[2,128,512]{2,1,0:T(8,128)S(1)}, u32[]{:S(2)}, u32[]{:S(2)}) collective-permute-start(f32[2,128,512]{2,1,0:T(8,128)S(1)} %get-tuple-element.18), channel_id=1, source_target_pairs={{8,0},{16,8},{24,16},{9,1},{17,9},{25,17},{10,2},{18,10},{26,18},{... | collective-permute-start | bytes 1572872 | tf_op jit(solution)/shard_map/ppermute | solution.py:23
  45.9 7.8 %middle0.1.body = f32[2,768,512]{2,1,0:T(8,128)S(1)} custom-call(s32[3]{0:T(128)S(1)} %pad_add_fusion.cols_ref, f32[2,2,768,768]{3,2,1,0:T(8,128)} %tile.7, f32[2,768,128]{2,1,0:T(8,128)S(1)} %collective-permute-done.6.lt.lb.left, f32[2,768,128]{2,1,0:T(8,128)S(1)} %collective-permute-done.7.rt.rb.right), custom_call_target="tpu_custom_call" | custom-call | bytes 9437184 | tf_op jit(solution)/shard_map/middle0/pallas_call | solution.py:101
  55.3 7.9 %middle1.1.body = f32[2,768,512]{2,1,0:T(8,128)S(1)} custom-call(s32[3]{0:T(128)S(1)} %pad_add_fusion.cols_ref, f32[2,2,768,768]{3,2,1,0:T(8,128)} %tile.7, f32[2,768,128]{2,1,0:T(8,128)S(1)} %collective-permute-done.2.lt.lb.left, f32[2,768,128]{2,1,0:T(8,128)S(1)} %collective-permute-done.3.rt.rb.right), custom_call_target="tpu_custom_call" | custom-call | bytes 9437184 | tf_op jit(solution)/shard_map/middle1/pallas_call | solution.py:101
  64.9 11.5 %first.1.psi = f32[2,512,512]{2,1,0:T(8,128)S(1)} custom-call(s32[1]{0:T(128)} %bitcast.2.rows_ref, f32[2,128,512]{2,1,0:T(8,128)S(1)} %collective-permute-done.8.top, f32[2,768,512]{2,1,0:T(8,128)} %copy-done.1, f32[2,128,512]{2,1,0:T(8,128)S(1)} %collective-permute-done.9.bottom, f32[2,512,512]{2,1,0:T(8,128)} %probe.3, f32[2,512,512]{2,1,0:T(8,128)} %pad_maximum_fusion.k, ...), custom_call_target="tpu_custom_call" | custom-call | flops 4294967296 | bytes 12582912 | tf_op jit(solution)/shard_map/first/pallas_call | solution.py:363
  76.4 15.1 %second.1 = (f32[2,1032,512]{2,1,0:T(8,128)}, bf16[1024,512]{1,0:T(8,128)(2,1)S(1)}) custom-call(s32[1]{0:T(128)} %bitcast.2.rows_ref, s32[1]{0:T(128)} %bitcast.17.count_ref, f32[2,128,512]{2,1,0:T(8,128)S(1)} %collective-permute-done.4.top, f32[2,768,512]{2,1,0:T(8,128)} %copy-done, f32[2,128,512]{2,1,0:T(8,128)S(1)} %collective-permute-done.5.bottom, ...), custom_call_target="tpu_custom_call" | custom-call | flops 4294967296 | bytes 14680064 | tf_op jit(solution)/shard_map/second/pallas_call | solution.py:372
  92.8 4.3 %collective-permute-start.13 = (f32[2,128,512]{2,1,0:T(8,128)S(1)}, f32[2,128,512]{2,1,0:T(8,128)S(1)}, u32[]{:S(2)}, u32[]{:S(2)}) collective-permute-start(f32[2,128,512]{2,1,0:T(8,128)S(1)} %get-tuple-element.33), channel_id=1, source_target_pairs={{8,0},{16,8},{24,16},{9,1},{17,9},{25,17},{10,2},{18,10},{26,18},{... | collective-permute-start | bytes 1572872 | tf_op jit(solution)/shard_map/ppermute | solution.py:23
  98.6 12.1 %third.1.grad = f32[2,1032,512]{2,1,0:T(8,128)} custom-call(s32[1]{0:T(128)} %bitcast.2.rows_ref, s32[1]{0:T(128)} %bitcast.18.count_ref, bf16[1024,512]{1,0:T(8,128)(2,1)S(1)} %get-tuple-element.21.back, f32[2,512,512]{2,1,0:T(8,128)S(1)} %copy-done.3, f32[2,512,512]{2,1,0:T(8,128)} %pad_maximum_fusion.k, bf16[512,512]{1,0:T(8,128)(2,1)S(1)} %copy-done.6, ...), custom_call_target="tpu_custom_call" | custom-call | flops 4294967296 | bytes 12582912 | tf_op jit(solution)/shard_map/third/pallas_call | solution.py:381
  111.9 4.0 %collective-permute-start.11 = (f32[2,128,512]{2,1,0:T(8,128)S(1)}, f32[2,128,512]{2,1,0:T(8,128)S(1)}, u32[]{:S(2)}, u32[]{:S(2)}) collective-permute-start(f32[2,128,512]{2,1,0:T(8,128)S(1)} %get-tuple-element.35), channel_id=1, source_target_pairs={{8,0},{16,8},{24,16},{9,1},{17,9},{25,17},{10,2},{18,10},{26,18},{... | collective-permute-start | bytes 1572872 | tf_op jit(solution)/shard_map/ppermute | solution.py:23
  118.6 8.3 %place1.1 = (f32[2,2,768,768]{3,2,1,0:T(8,128)}, f32[2,768,128]{2,1,0:T(8,128)S(1)}, f32[2,768,128]{2,1,0:T(8,128)S(1)}) custom-call(s32[3]{0:T(128)S(1)} %pad_add_fusion.cols_ref, f32[2]{0:T(128)S(1)} %copy-done.2, f32[2,1032,512]{2,1,0:T(8,128)} %get-tuple-element.22.grad, f32[2,128,512]{2,1,0:T(8,128)S(1)} %collective-permute-done.12.above, ...), custom_call_target="tpu_custom_call" | custom-call | bytes 14680064 | tf_op jit(solution)/shard_map/place1/pallas_call | solution.py:291
  126.9 7.8 %collective-permute-start.16 = (f32[2,768,128]{2,1,0:T(8,128)S(1)}, f32[2,768,128]{2,1,0:T(8,128)S(1)}, u32[]{:S(2)}, u32[]{:S(2)}) collective-permute-start(f32[2,768,128]{2,1,0:T(8,128)S(1)} %get-tuple-element.26), channel_id=1, source_target_pairs={{0,1},{1,2},{2,3},{3,4},{4,5},{5,6},{6,7},{8,9},{9,10},{10,11},{11... | collective-permute-start | bytes 2359304 | tf_op jit(solution)/shard_map/ppermute | solution.py:23
  136.6 4.5 %collective-permute-done.10.above = f32[2,128,512]{2,1,0:T(8,128)S(1)} collective-permute-done((f32[2,128,512]{2,1,0:T(8,128)S(1)}, f32[2,128,512]{2,1,0:T(8,128)S(1)}, u32[]{:S(2)}, u32[]{:S(2)}) %collective-permute-start.10) | collective-permute-done | bytes 524320 | tf_op jit(solution)/shard_map/ppermute | solution.py:23
  141.1 8.3 %place0.1 = (f32[2,2,768,768]{3,2,1,0:T(8,128)}, f32[2,768,128]{2,1,0:T(8,128)S(1)}, f32[2,768,128]{2,1,0:T(8,128)S(1)}) custom-call(s32[3]{0:T(128)S(1)} %pad_add_fusion.cols_ref, f32[2]{0:T(128)S(1)} %copy-done.2, f32[2,1032,512]{2,1,0:T(8,128)} %third.1.grad, f32[2,128,512]{2,1,0:T(8,128)S(1)} %collective-permute-done.10.above, ...), custom_call_target="tpu_custom_call", output_to_operand_aliasing={{0}: (6, {})} | custom-call | bytes 14680064 | tf_op jit(solution)/shard_map/place0/pallas_call | solution.py:291
  149.3 5.7 %collective-permute-start.14 = (f32[2,768,128]{2,1,0:T(8,128)S(1)}, f32[2,768,128]{2,1,0:T(8,128)S(1)}, u32[]{:S(2)}, u32[]{:S(2)}) collective-permute-start(f32[2,768,128]{2,1,0:T(8,128)S(1)} %get-tuple-element.24), channel_id=1, source_target_pairs={{0,1},{1,2},{2,3},{3,4},{4,5},{5,6},{6,7},{8,9},{9,10},{10,11},{11... | collective-permute-start | bytes 2359304 | tf_op jit(solution)/shard_map/ppermute | solution.py:23
  156.9 3.7 %border1.1.old = f32[2,2,768,768]{3,2,1,0:T(8,128)} custom-call(f32[2]{0:T(128)S(1)} %copy-done.2, f32[2,768,128]{2,1,0:T(8,128)S(1)} %collective-permute-done.16.left, f32[2,768,128]{2,1,0:T(8,128)S(1)} %collective-permute-done.17.right, f32[2,2,768,768]{3,2,1,0:T(8,128)} %get-tuple-element.28.old), custom_call_target="tpu_custom_call", output_to_operand_aliasing={{}: (3, {})} | custom-call | bytes 5242880 | tf_op jit(solution)/shard_map/border1/pallas_call | solution.py:324
  160.6 3.3 %collective-permute-done.14.left = f32[2,768,128]{2,1,0:T(8,128)S(1)} collective-permute-done((f32[2,768,128]{2,1,0:T(8,128)S(1)}, f32[2,768,128]{2,1,0:T(8,128)S(1)}, u32[]{:S(2)}, u32[]{:S(2)}) %collective-permute-start.14) | collective-permute-done | bytes 786464 | tf_op jit(solution)/shard_map/ppermute | solution.py:23
  163.9 4.4 %collective-permute-done.15.right = f32[2,768,128]{2,1,0:T(8,128)S(1)} collective-permute-done((f32[2,768,128]{2,1,0:T(8,128)S(1)}, f32[2,768,128]{2,1,0:T(8,128)S(1)}, u32[]{:S(2)}, u32[]{:S(2)}) %collective-permute-start.15) | collective-permute-done | bytes 786464 | tf_op jit(solution)/shard_map/ppermute | solution.py:23
  168.3 3.7 %border0.1 = f32[2,2,768,768]{3,2,1,0:T(8,128)} custom-call(f32[2]{0:T(128)S(1)} %copy-done.2, f32[2,768,128]{2,1,0:T(8,128)S(1)} %collective-permute-done.14.left, f32[2,768,128]{2,1,0:T(8,128)S(1)} %collective-permute-done.15.right, f32[2,2,768,768]{3,2,1,0:T(8,128)} %border1.1.old), custom_call_target="tpu_custom_call", output_to_operand_aliasing={{}: (3, {})} | custom-call | bytes 5242880 | tf_op jit(solution)/shard_map/border0/pallas_call | solution.py:324
  (50 shorter events, 31.0 us)
Async XLA Ops:
  0.0 13.4 %copy-start.8 = (s32[1,1,1,2]{3,2,1,0:T(1,128)S(1)}, s32[1,1,1,2]{3,2,1,0:T(1,128)}, u32[]{:S(2)}) copy-start(s32[1,1,1,2]{3,2,1,0:T(1,128)} %param.13) | copy-start | bytes 28
  2.1 22.0 %collective-permute-start.7 = (f32[2,768,128]{2,1,0:T(8,128)S(1)}, f32[2,768,128]{2,1,0:T(8,128)S(1)}, u32[]{:S(2)}, u32[]{:S(2)}) collective-permute-start(f32[2,768,128]{2,1,0:T(8,128)S(1)} %get-tuple-element.29), channel_id=1, source_target_pairs={{1,0},{2,1},{3,2},{4,3},{5,4},{6,5},{7,6},{9,8},{10,9},{11,10},{12... | collective-permute-start | bytes 2359304 | tf_op jit(solution)/shard_map/ppermute | solution.py:23
  4.7 19.4 %collective-permute-start.6 = (f32[2,768,128]{2,1,0:T(8,128)S(1)}, f32[2,768,128]{2,1,0:T(8,128)S(1)}, u32[]{:S(2)}, u32[]{:S(2)}) collective-permute-start(f32[2,768,128]{2,1,0:T(8,128)S(1)} %get-tuple-element.30), channel_id=1, source_target_pairs={{0,1},{1,2},{2,3},{3,4},{4,5},{5,6},{6,7},{8,9},{9,10},{10,11},{11... | collective-permute-start | bytes 2359304 | tf_op jit(solution)/shard_map/ppermute | solution.py:23
  7.8 28.5 %collective-permute-start.3 = (f32[2,768,128]{2,1,0:T(8,128)S(1)}, f32[2,768,128]{2,1,0:T(8,128)S(1)}, u32[]{:S(2)}, u32[]{:S(2)}) collective-permute-start(f32[2,768,128]{2,1,0:T(8,128)S(1)} %get-tuple-element.31), channel_id=1, source_target_pairs={{1,0},{2,1},{3,2},{4,3},{5,4},{6,5},{7,6},{9,8},{10,9},{11,10},{12... | collective-permute-start | bytes 2359304 | tf_op jit(solution)/shard_map/ppermute | solution.py:23
  9.8 26.6 %collective-permute-start.2 = (f32[2,768,128]{2,1,0:T(8,128)S(1)}, f32[2,768,128]{2,1,0:T(8,128)S(1)}, u32[]{:S(2)}, u32[]{:S(2)}) collective-permute-start(f32[2,768,128]{2,1,0:T(8,128)S(1)} %get-tuple-element.32), channel_id=1, source_target_pairs={{0,1},{1,2},{2,3},{3,4},{4,5},{5,6},{6,7},{8,9},{9,10},{10,11},{11... | collective-permute-start | bytes 2359304 | tf_op jit(solution)/shard_map/ppermute | solution.py:23
  13.4 2.9 %collective-permute-start.1 = (s32[2]{0:T(128)S(1)}, s32[2]{0:T(128)S(1)}, u32[]{:S(2)}, u32[]{:S(2)}) collective-permute-start(s32[2]{0:T(128)S(1)} %bitcast.20), channel_id=1, source_target_pairs={{8,0},{16,8},{24,16},{9,1},{17,9},{25,17},{10,2},{18,10},{26,18},{... | collective-permute-start | bytes 32 | tf_op jit(solution)/shard_map/ppermute | solution.py:23
  16.3 5.1 %collective-permute-start = (s32[2]{0:T(128)S(1)}, s32[2]{0:T(128)S(1)}, u32[]{:S(2)}, u32[]{:S(2)}) collective-permute-start(s32[2]{0:T(128)S(1)} %bitcast.21), channel_id=1, source_target_pairs={{0,8},{8,16},{16,24},{1,9},{9,17},{17,25},{2,10},{10,18},{18,26},{... | collective-permute-start | bytes 32 | tf_op jit(solution)/shard_map/ppermute | solution.py:23
  26.0 38.8 %collective-permute-start.8 = (f32[2,128,512]{2,1,0:T(8,128)S(1)}, f32[2,128,512]{2,1,0:T(8,128)S(1)}, u32[]{:S(2)}, u32[]{:S(2)}) collective-permute-start(f32[2,128,512]{2,1,0:T(8,128)S(1)} %get-tuple-element.19), channel_id=1, source_target_pairs={{0,8},{8,16},{16,24},{1,9},{9,17},{17,25},{2,10},{10,18},{18,26},{... | collective-permute-start | bytes 1572872 | tf_op jit(solution)/shard_map/ppermute | solution.py:23
  27.3 37.5 %collective-permute-start.9 = (f32[2,128,512]{2,1,0:T(8,128)S(1)}, f32[2,128,512]{2,1,0:T(8,128)S(1)}, u32[]{:S(2)}, u32[]{:S(2)}) collective-permute-start(f32[2,128,512]{2,1,0:T(8,128)S(1)} %get-tuple-element.20), channel_id=1, source_target_pairs={{8,0},{16,8},{24,16},{9,1},{17,9},{25,17},{10,2},{18,10},{26,18},{... | collective-permute-start | bytes 1572872 | tf_op jit(solution)/shard_map/ppermute | solution.py:23
  38.2 38.2 %collective-permute-start.4 = (f32[2,128,512]{2,1,0:T(8,128)S(1)}, f32[2,128,512]{2,1,0:T(8,128)S(1)}, u32[]{:S(2)}, u32[]{:S(2)}) collective-permute-start(f32[2,128,512]{2,1,0:T(8,128)S(1)} %get-tuple-element.17), channel_id=1, source_target_pairs={{0,8},{8,16},{16,24},{1,9},{9,17},{17,25},{2,10},{10,18},{18,26},{... | collective-permute-start | bytes 1572872 | tf_op jit(solution)/shard_map/ppermute | solution.py:23
  39.5 36.9 %collective-permute-start.5 = (f32[2,128,512]{2,1,0:T(8,128)S(1)}, f32[2,128,512]{2,1,0:T(8,128)S(1)}, u32[]{:S(2)}, u32[]{:S(2)}) collective-permute-start(f32[2,128,512]{2,1,0:T(8,128)S(1)} %get-tuple-element.18), channel_id=1, source_target_pairs={{8,0},{16,8},{24,16},{9,1},{17,9},{25,17},{10,2},{18,10},{26,18},{... | collective-permute-start | bytes 1572872 | tf_op jit(solution)/shard_map/ppermute | solution.py:23
  55.3 9.5 %copy-start.5 = (bf16[512,512]{1,0:T(8,128)(2,1)S(1)}, bf16[512,512]{1,0:T(8,128)(2,1)}, u32[]{:S(2)}) copy-start(bf16[512,512]{1,0:T(8,128)(2,1)} %constant.5.clone.sin) | copy-start | bytes 1572868
  55.3 9.5 %copy-start.6 = (bf16[512,512]{1,0:T(8,128)(2,1)S(1)}, bf16[512,512]{1,0:T(8,128)(2,1)}, u32[]{:S(2)}) copy-start(bf16[512,512]{1,0:T(8,128)(2,1)} %constant.4.clone.cos) | copy-start | bytes 1572868
  64.9 11.5 %copy-start.4 = (bf16[1,1,1,512,512]{4,3,2,1,0:T(8,128)(2,1)S(1)}, bf16[1,1,1,512,512]{4,3,2,1,0:T(8,128)(2,1)}, u32[]{:S(2)}) copy-start(bf16[1,1,1,512,512]{4,3,2,1,0:T(8,128)(2,1)} %param.12) | copy-start | bytes 1572868
  76.4 22.2 %copy-start.3 = (f32[2,512,512]{2,1,0:T(8,128)S(1)}, f32[2,512,512]{2,1,0:T(8,128)}, u32[]{:S(2)}) copy-start(f32[2,512,512]{2,1,0:T(8,128)} %probe.3) | copy-start | bytes 6291460
  92.8 24.5 %collective-permute-start.13 = (f32[2,128,512]{2,1,0:T(8,128)S(1)}, f32[2,128,512]{2,1,0:T(8,128)S(1)}, u32[]{:S(2)}, u32[]{:S(2)}) collective-permute-start(f32[2,128,512]{2,1,0:T(8,128)S(1)} %get-tuple-element.33), channel_id=1, source_target_pairs={{8,0},{16,8},{24,16},{9,1},{17,9},{25,17},{10,2},{18,10},{26,18},{... | collective-permute-start | bytes 1572872 | tf_op jit(solution)/shard_map/ppermute | solution.py:23
  97.1 21.5 %collective-permute-start.12 = (f32[2,128,512]{2,1,0:T(8,128)S(1)}, f32[2,128,512]{2,1,0:T(8,128)S(1)}, u32[]{:S(2)}, u32[]{:S(2)}) collective-permute-start(f32[2,128,512]{2,1,0:T(8,128)S(1)} %get-tuple-element.34), channel_id=1, source_target_pairs={{0,8},{8,16},{16,24},{1,9},{9,17},{17,25},{2,10},{10,18},{18,26},{... | collective-permute-start | bytes 1572872 | tf_op jit(solution)/shard_map/ppermute | solution.py:23
  98.5 20.1 %copy-start.2 = (f32[2]{0:T(128)S(1)}, f32[2]{0:T(128)}, u32[]{:S(2)}) copy-start(f32[2]{0:T(128)} %step_ref.7) | copy-start | bytes 28
  111.9 24.7 %collective-permute-start.11 = (f32[2,128,512]{2,1,0:T(8,128)S(1)}, f32[2,128,512]{2,1,0:T(8,128)S(1)}, u32[]{:S(2)}, u32[]{:S(2)}) collective-permute-start(f32[2,128,512]{2,1,0:T(8,128)S(1)} %get-tuple-element.35), channel_id=1, source_target_pairs={{8,0},{16,8},{24,16},{9,1},{17,9},{25,17},{10,2},{18,10},{26,18},{... | collective-permute-start | bytes 1572872 | tf_op jit(solution)/shard_map/ppermute | solution.py:23
  116.0 25.1 %collective-permute-start.10 = (f32[2,128,512]{2,1,0:T(8,128)S(1)}, f32[2,128,512]{2,1,0:T(8,128)S(1)}, u32[]{:S(2)}, u32[]{:S(2)}) collective-permute-start(f32[2,128,512]{2,1,0:T(8,128)S(1)} %get-tuple-element.36), channel_id=1, source_target_pairs={{0,8},{8,16},{16,24},{1,9},{9,17},{17,25},{2,10},{10,18},{18,26},{... | collective-permute-start | bytes 1572872 | tf_op jit(solution)/shard_map/ppermute | solution.py:23
  126.9 30.1 %collective-permute-start.16 = (f32[2,768,128]{2,1,0:T(8,128)S(1)}, f32[2,768,128]{2,1,0:T(8,128)S(1)}, u32[]{:S(2)}, u32[]{:S(2)}) collective-permute-start(f32[2,768,128]{2,1,0:T(8,128)S(1)} %get-tuple-element.26), channel_id=1, source_target_pairs={{0,1},{1,2},{2,3},{3,4},{4,5},{5,6},{6,7},{8,9},{9,10},{10,11},{11... | collective-permute-start | bytes 2359304 | tf_op jit(solution)/shard_map/ppermute | solution.py:23
  134.7 22.3 %collective-permute-start.17 = (f32[2,768,128]{2,1,0:T(8,128)S(1)}, f32[2,768,128]{2,1,0:T(8,128)S(1)}, u32[]{:S(2)}, u32[]{:S(2)}) collective-permute-start(f32[2,768,128]{2,1,0:T(8,128)S(1)} %get-tuple-element.27), channel_id=1, source_target_pairs={{1,0},{2,1},{3,2},{4,3},{5,4},{6,5},{7,6},{9,8},{10,9},{11,10},{12... | collective-permute-start | bytes 2359304 | tf_op jit(solution)/shard_map/ppermute | solution.py:23
  149.3 14.6 %collective-permute-start.14 = (f32[2,768,128]{2,1,0:T(8,128)S(1)}, f32[2,768,128]{2,1,0:T(8,128)S(1)}, u32[]{:S(2)}, u32[]{:S(2)}) collective-permute-start(f32[2,768,128]{2,1,0:T(8,128)S(1)} %get-tuple-element.24), channel_id=1, source_target_pairs={{0,1},{1,2},{2,3},{3,4},{4,5},{5,6},{6,7},{8,9},{9,10},{10,11},{11... | collective-permute-start | bytes 2359304 | tf_op jit(solution)/shard_map/ppermute | solution.py:23
  155.0 13.3 %collective-permute-start.15 = (f32[2,768,128]{2,1,0:T(8,128)S(1)}, f32[2,768,128]{2,1,0:T(8,128)S(1)}, u32[]{:S(2)}, u32[]{:S(2)}) collective-permute-start(f32[2,768,128]{2,1,0:T(8,128)S(1)} %get-tuple-element.25), channel_id=1, source_target_pairs={{1,0},{2,1},{3,2},{4,3},{5,4},{6,5},{7,6},{9,8},{10,9},{11,10},{12... | collective-permute-start | bytes 2359304 | tf_op jit(solution)/shard_map/ppermute | solution.py:23
  (3 other events, 11.8 us)

commit v2 on v1

--- a/solution.py
+++ b/solution.py
@@ -56,42 +56,42 @@
     inner = top.shape[-1]
     width = up.shape[-1]
     for left, tile, right, out, which in ((lt, top, rt, up, 1), (lb, bottom, rb, down, 2)):
-        wide[:, :H] = left[0]
+        wide[:, :H] = left[0, 0]
         wide[:, H : H + inner] = tile[0, 0]
-        wide[:, H + inner : 2 * H + inner] = right[0]
+        wide[:, H + inner : 2 * H + inner] = right[0, 0]
         wide[:, 2 * H + inner :] = jnp.zeros((wide.shape[0], LANES), F32)
-        out[0] = take_columns(wide, cols_ref[which], width)
-
-
-def edges(cols, tile, left, right, s, width):
+        out[0, 0] = take_columns(wide, cols_ref[which], width)
+
+
+def edges(cols, tile, left, right, width):
     rows, inner = tile.shape[2:]
     last = rows // H - 1
-    side = lambda r: pl.BlockSpec((1, H, H), lambda c: (c, r, 0))
+    side = lambda r: pl.BlockSpec((1, 1, H, H), lambda s, c: (s, c, r, 0))
     return pl.pallas_call(
         edges_kernel,
-        grid=(2,),
+        grid=(2, 2),
         in_specs=[
             SMEM,
-            pl.BlockSpec((1, 1, H, inner), lambda c: (s, c, 0, 0)),
-            pl.BlockSpec((1, 1, H, inner), lambda c: (s, c, last, 0)),
+            pl.BlockSpec((1, 1, H, inner), lambda s, c: (s, c, 0, 0)),
+            pl.BlockSpec((1, 1, H, inner), lambda s, c: (s, c, last, 0)),
             side(0),
             side(last),
             side(0),
             side(last),
         ],
-        out_specs=[pl.BlockSpec((1, H, width), lambda c: (c, 0, 0))] * 2,
-        out_shape=[jax.ShapeDtypeStruct((2, H, width), F32)] * 2,
+        out_specs=[pl.BlockSpec((1, 1, H, width), lambda s, c: (s, c, 0, 0))] * 2,
+        out_shape=[jax.ShapeDtypeStruct((2, 2, H, width), F32)] * 2,
         scratch_shapes=[pltpu.VMEM((H, inner + 2 * H + LANES), F32)],
-        name=f"edges{s}",
-        **params(0, 3 << 20),
+        name="edges",
+        **params(0, 5 << 20),
     )(cols, tile, tile, left, left, right, right)
 
 
 def middle_kernel(cols_ref, tile, left, right, out, wide):
     inner = tile.shape[-1]
-    wide[:, :H] = left[0]
+    wide[:, :H] = left[0, 0]
     wide[:, H : H + inner] = tile[0, 0]
-    wide[:, H + inner : 2 * H + inner] = right[0]
+    wide[:, H + inner : 2 * H + inner] = right[0, 0]
     wide[:, 2 * H + inner :] = jnp.zeros((wide.shape[0], LANES), F32)
     out[0] = take_columns(wide, cols_ref[0], out.shape[-1])
 
@@ -100,16 +100,16 @@
     rows, inner = tile.shape[2:]
     return pl.pallas_call(
         middle_kernel,
-        grid=(2, rows // H),
+        grid=(2,),
         in_specs=[
             SMEM,
-            pl.BlockSpec((1, 1, H, inner), lambda c, r: (s, c, r, 0)),
-            pl.BlockSpec((1, H, H), lambda c, r: (c, r, 0)),
-            pl.BlockSpec((1, H, H), lambda c, r: (c, r, 0)),
+            pl.BlockSpec((1, 1, rows, inner), lambda c: (s, c, 0, 0)),
+            pl.BlockSpec((1, 1, rows, H), lambda c: (s, c, 0, 0)),
+            pl.BlockSpec((1, 1, rows, H), lambda c: (s, c, 0, 0)),
         ],
-        out_specs=pl.BlockSpec((1, H, width), lambda c, r: (c, r, 0)),
+        out_specs=pl.BlockSpec((1, rows, width), lambda c: (c, 0, 0)),
         out_shape=jax.ShapeDtypeStruct((2, rows, width), F32),
-        scratch_shapes=[pltpu.VMEM((H, inner + 2 * H + LANES), F32)],
+        scratch_shapes=[pltpu.VMEM((rows, inner + 2 * H + LANES), F32)],
         name=f"middle{s}",
         **params(0, 9 << 20),
     )(cols, tile, left, right)
@@ -259,9 +259,8 @@
     ]
 
 
-def place_kernel(s, cols_ref, step_ref, grad, above, below, tile, *rest):
-    out, to_left, to_right, wide = rest[-4:]
-    rows, inner = tile.shape[2:]
+def gather(cols_ref, grad, above, below, wide):
+    rows = wide.shape[0]
     width = grad.shape[-1]
     wide[...] = jnp.zeros_like(wide)
 
@@ -276,61 +275,61 @@
 
     add(0, above[0], cols_ref[1])
     add(rows - H, below[0], cols_ref[2])
-    out[0, 0] = tile[0, 0] - step_ref[s] * wide[:, H : H + inner]
+
+
+def spill_kernel(cols_ref, grad, above, below, to_left, to_right, wide):
+    inner = wide.shape[1] - 2 * H - LANES
+    gather(cols_ref, grad, above, below, wide)
     to_left[0] = wide[:, :H]
     to_right[0] = wide[:, H + inner : 2 * H + inner]
 
 
-def place(cols, step, grad, above, below, tile, s, so_far):
+def place_kernel(s, cols_ref, step_ref, grad, above, below, left, right, tile, *rest):
+    out, wide = rest[-2:]
+    inner = tile.shape[-1]
+    gather(cols_ref, grad, above, below, wide)
+    wide[:, H : 2 * H] += left[0]
+    wide[:, inner : H + inner] += right[0]
+    out[0, 0] = tile[0, 0] - step_ref[s] * wide[:, H : H + inner]
+
+
+def gradient_specs(grad, rows):
+    edge = pl.BlockSpec((1, H, grad.shape[-1]), lambda c: (c, 0, 0))
+    side = pl.BlockSpec((1, rows, H), lambda c: (c, 0, 0))
+    return [pl.BlockSpec((1,) + grad.shape[1:], lambda c: (c, 0, 0)), edge, edge], [side, side]
+
+
+def spill(cols, grad, above, below, tile, s):
     rows, inner = tile.shape[2:]
-    width = grad.shape[-1]
+    sources, sides = gradient_specs(grad, rows)
+    return pl.pallas_call(
+        spill_kernel,
+        grid=(2,),
+        in_specs=[SMEM] + sources,
+        out_specs=sides,
+        out_shape=[jax.ShapeDtypeStruct((2, rows, H), F32)] * 2,
+        scratch_shapes=[pltpu.VMEM((rows, inner + 2 * H + LANES), F32)],
+        name=f"spill{s}",
+        **params(0, 7 << 20),
+    )(cols, grad, above, below)
+
+
+def place(cols, step, grad, above, below, left, right, tile, s, so_far):
+    rows, inner = tile.shape[2:]
+    sources, sides = gradient_specs(grad, rows)
     plane = pl.BlockSpec((1, 1, rows, inner), lambda c: (s, c, 0, 0))
-    edge = pl.BlockSpec((1, H, width), lambda c: (c, 0, 0))
-    side = pl.BlockSpec((1, rows, H), lambda c: (c, 0, 0))
     more = [] if so_far is None else [so_far]
     return pl.pallas_call(
         functools.partial(place_kernel, s),
         grid=(2,),
-        in_specs=[SMEM, SMEM, pl.BlockSpec((1,) + grad.shape[1:], lambda c: (c, 0, 0)), edge, edge, plane]
-        + [pl.BlockSpec(memory_space=pl.ANY)] * len(more),
-        out_specs=[plane, side, side],
-        out_shape=[
-            jax.ShapeDtypeStruct(tile.shape, F32),
-            jax.ShapeDtypeStruct((2, rows, H), F32),
-            jax.ShapeDtypeStruct((2, rows, H), F32),
-        ],
+        in_specs=[SMEM, SMEM] + sources + sides + [plane] + [pl.BlockSpec(memory_space=pl.ANY)] * len(more),
+        out_specs=plane,
+        out_shape=jax.ShapeDtypeStruct(tile.shape, F32),
         scratch_shapes=[pltpu.VMEM((rows, inner + 2 * H + LANES), F32)],
-        input_output_aliases={6: 0} if more else {},
+        input_output_aliases={8: 0} if more else {},
         name=f"place{s}",
         **params(0, 14 << 20),
-    )(cols, step, grad, above, below, tile, *more)
-
-
-def border_kernel(s, step_ref, left, right, old, out):
-    @pl.when(pl.program_id(1) == 0)
-    def _():
-        out[0, 0] = old[0, 0] - step_ref[s] * left[0]
-
-    @pl.when(pl.program_id(1) == 1)
-    def _():
-        out[0, 0] = old[0, 0] - step_ref[s] * right[0]
-
-
-def border(step, left, right, out, s):
-    rows, inner = out.shape[2:]
-    far = inner // H - 1
-    strip = pl.BlockSpec((1, 1, rows, H), lambda c, e: (s, c, 0, e * far))
-    side = pl.BlockSpec((1, rows, H), lambda c, e: (c, 0, 0))
-    return pl.pallas_call(
-        functools.partial(border_kernel, s),
-        grid=(2, 2),
-        in_specs=[SMEM, side, side, strip],
-        out_specs=strip,
-        out_shape=jax.ShapeDtypeStruct(out.shape, F32),
-        input_output_aliases={3: 0},
-        name=f"border{s}",
-        **params(0, 5 << 20),
-    )(step, left, right, out)
+    )(cols, step, grad, above, below, left, right, tile, *more)
 
 
 def per_device(object_tiles, probe, prop_phase, amplitudes, offsets, counts, step_size):
@@ -345,16 +344,12 @@
     row = mine[:1]
     count = counts[0]
 
-    lefts, rights, tops, bottoms, bodies = [], [], [], [], []
-    for s in range(2):
-        lefts.append(shifted(object_tiles[s, :, :, inner - H :], "cols", 1))
-        rights.append(shifted(object_tiles[s, :, :, :H], "cols", -1))
-    for s in range(2):
-        up, down = edges(cols, object_tiles, lefts[s], rights[s], s, n)
-        tops.append(shifted(down, "rows", 1))
-        bottoms.append(shifted(up, "rows", -1))
-    for s in range(2):
-        bodies.append(middle(cols, object_tiles, lefts[s], rights[s], s, n))
+    left = shifted(object_tiles[:, :, :, inner - H :], "cols", 1)
+    right = shifted(object_tiles[:, :, :, :H], "cols", -1)
+    up, down = edges(cols, object_tiles, left, right, n)
+    tops = [shifted(down[s], "rows", 1) for s in range(2)]
+    bottoms = [shifted(up[s], "rows", -1) for s in range(2)]
+    bodies = [middle(cols, object_tiles, left, right, s, n) for s in range(2)]
 
     per_transform = 2 * 2 * (2 * n) * (2 * n) * n
     ext = jax.ShapeDtypeStruct((2, rows + 2 * H + SUBLANES, n), F32)
@@ -388,17 +383,16 @@
         **params(2 * per_transform, 12 << 20),
     )(row, count, back, probe, kernel, cos, sin)
 
-    out = None
-    sides = []
+    parts = []
     for s, grad in ((1, grad2), (0, grad1)):
         from_above = shifted(grad[:, rows + H : rows + 2 * H], "rows", 1)
         from_below = shifted(grad[:, :H], "rows", -1)
-        out, to_left, to_right = place(
-            cols, step_size, grad, from_above, from_below, object_tiles, s, out
-        )
-        sides.append((s, shifted(to_right, "cols", 1), shifted(to_left, "cols", -1)))
-    for s, left, right in sides:
-        out = border(step_size, left, right, out, s)
+        to_left, to_right = spill(cols, grad, from_above, from_below, object_tiles, s)
+        from_left, from_right = shifted(to_right, "cols", 1), shifted(to_left, "cols", -1)
+        parts.append((s, (grad, from_above, from_below, from_left, from_right)))
+    out = None
+    for s, pieces in parts:
+        out = place(cols, step_size, *pieces, object_tiles, s, out)
     return out
 
 

time: 173 us -> 175 us (1.012)
  waiting for transfers between devices: 16.8 us -> 21.8 us
  Pallas kernels: 81.9 us -> 78.7 us
  starting transfers between devices: 55.1 us -> 58.2 us
  local copies, waits for them, and re-layouts: 13.6 us -> 10.6 us
    ppermute x18 -> x16, waiting for transfers between devices: 16.8 us -> 21.8 us  [shifted(): return lax.ppermute(block, axis, route)]
    unnamed x18 -> x14, local copies, waits for them, and re-layouts: 3.32 us -> 0.03 us
    ppermute x18 -> x16, starting transfers between devices: 55.1 us -> 58.2 us  [shifted(): return lax.ppermute(block, axis, route)]
    pallas_call x6 -> x5, Pallas kernels: 26.7 us -> 23.9 us  [the longest x2 10.8 us: spill(): pl.pallas_call(spill_kernel, grid=(2,), in_specs=[SMEM] + sources, out_sp...]
    slice x0 -> x1, local copies, waits for them, and re-layouts: none -> 2.15 us  [per_device(): right = shifted(object_tiles[:, :, :, :H], 'cols', -1)]
    squeeze x1 -> x2, local copies, waits for them, and re-layouts: 2.12 us -> 0.14 us  [the longest x1 0.07 us: per_device(): tops = [shifted(down[s], 'rows', 1) for s in range(2)]]
  transfers between devices with their start and end apart: 18 -> 16, of which waited for: 6 -> 6; matrix products, arithmetic and copies ran while one was open for 6% -> 6% of each run, Pallas kernels for 37% -> 30%
where the time goes in v2:
time: 175 us; the launch traced here: 174 us
  Pallas kernels  78.7 us (45%)
  starting transfers between devices  58.2 us (33%)
  waiting for transfers between devices  21.8 us (12%)
  local copies, waits for them, and re-layouts  10.6 us (6%)
  other arithmetic  3.55 us (2%)
    ppermute x16, starting transfers between devices, shifted(): return lax.ppermute(block, axis, route)  58.2 us
    ppermute x16, waiting for transfers between devices, shifted(): return lax.ppermute(block, axis, route)  21.8 us
    pallas_call x2, Pallas kernels, place(): pl.pallas_call(functools.partial(place_kernel, s), grid=(2,), in_specs=[S...  16.7 us
    pallas_call x1, Pallas kernels, per_device(): pl.pallas_call(second_kernel, in_specs=[SMEM] * 2 + [VMEM] * 7, out_specs...  14.9 us
    pallas_call x1, Pallas kernels, per_device(): pl.pallas_call(third_kernel, in_specs=[SMEM] * 2 + [VMEM] * 5, out_specs=...  11.9 us
    pallas_call x1, Pallas kernels, per_device(): pl.pallas_call(first_kernel, in_specs=[SMEM] + [VMEM] * 7, out_specs=VMEM...  11.3 us
    pallas_call x2, Pallas kernels, spill(): pl.pallas_call(spill_kernel, grid=(2,), in_specs=[SMEM] + sources, out_sp...  10.8 us
    pallas_call x2, Pallas kernels, middle(): pl.pallas_call(middle_kernel, grid=(2,), in_specs=[SMEM, pl.BlockSpec((1,...  9.79 us
  transfers between devices with their start and end apart: 16, of which 6 were waited for; matrix products, arithmetic and copies ran while one was open for 6% of the time, Pallas kernels for 30%

profile of v2, /device:TPU:15, one launch (start us, length us, event | category | flops | bytes accessed | tf_op | source)
XLA Modules:
  0.0 173.8 jit_solution(7428660840183297963)
XLA Ops:
  2.2 2.6 %collective-permute-start.3 = (f32[2,2,768,128]{3,2,1,0:T(8,128)S(1)}, f32[2,2,768,128]{3,2,1,0:T(8,128)S(1)}, u32[]{:S(2)}, u32[]{:S(2)}) collective-permute-start(f32[2,2,768,128]{3,2,1,0:T(8,128)S(1)} %get-tuple-element.21), channel_id=1, source_target_pairs={{1,0},{2,1},{3,2},{4,3},{5,4},{6,5},{7,6},{9,8},{10,9},{11,10},{12... | collective-permute-start | bytes 4718600 | tf_op jit(solution)/shard_map/ppermute | solution.py:23
  4.7 3.1 %collective-permute-start.2 = (f32[2,2,768,128]{3,2,1,0:T(8,128)S(1)}, f32[2,2,768,128]{3,2,1,0:T(8,128)S(1)}, u32[]{:S(2)}, u32[]{:S(2)}) collective-permute-start(f32[2,2,768,128]{3,2,1,0:T(8,128)S(1)} %get-tuple-element.22), channel_id=1, source_target_pairs={{0,1},{1,2},{2,3},{3,4},{4,5},{5,6},{6,7},{8,9},{9,10},{10,11},{11... | collective-permute-start | bytes 4718600 | tf_op jit(solution)/shard_map/ppermute | solution.py:23
  7.9 2.2 %collective-permute-start.1 = (s32[2]{0:T(128)S(1)}, s32[2]{0:T(128)S(1)}, u32[]{:S(2)}, u32[]{:S(2)}) collective-permute-start(s32[2]{0:T(128)S(1)} %bitcast.20), channel_id=1, source_target_pairs={{8,0},{16,8},{24,16},{9,1},{17,9},{25,17},{10,2},{18,10},{26,18},{... | collective-permute-start | bytes 32 | tf_op jit(solution)/shard_map/ppermute | solution.py:23
  17.2 7.1 %collective-permute-done.3.rt.rb.right = f32[2,2,768,128]{3,2,1,0:T(8,128)S(1)} collective-permute-done((f32[2,2,768,128]{3,2,1,0:T(8,128)S(1)}, f32[2,2,768,128]{3,2,1,0:T(8,128)S(1)}, u32[]{:S(2)}, u32[]{:S(2)}) %collective-permute-start.3) | collective-permute-done | bytes 1572896 | tf_op jit(solution)/shard_map/ppermute | solution.py:23
  25.2 3.3 %edges.1 = (f32[2,2,128,512]{3,2,1,0:T(8,128)S(1)}, f32[2,2,128,512]{3,2,1,0:T(8,128)S(1)}) custom-call(s32[3]{0:T(128)S(1)} %pad_add_fusion.cols_ref, f32[2,2,768,768]{3,2,1,0:T(8,128)} %tile.7, f32[2,2,768,768]{3,2,1,0:T(8,128)} %tile.7, f32[2,2,768,128]{3,2,1,0:T(8,128)S(1)} %collective-permute-done.2.lt.lb.left, ...), custom_call_target="tpu_custom_call" | custom-call | bytes 5242880 | tf_op jit(solution)/shard_map/edges/pallas_call | solution.py:70
  30.1 4.0 %collective-permute-start.7 = (f32[2,128,512]{2,1,0:T(8,128)S(1)}, f32[2,128,512]{2,1,0:T(8,128)S(1)}, u32[]{:S(2)}, u32[]{:S(2)}) collective-permute-start(f32[2,128,512]{2,1,0:T(8,128)S(1)} %get-tuple-element.29), channel_id=1, source_target_pairs={{8,0},{16,8},{24,16},{9,1},{17,9},{25,17},{10,2},{18,10},{26,18},{... | collective-permute-start | bytes 1572872 | tf_op jit(solution)/shard_map/ppermute | solution.py:23
  34.8 3.7 %cosine_bitcast_fusion = (f32[1,512,512]{2,1,0:T(8,128)S(1)}, f32[1,512,512]{2,1,0:T(8,128)S(1)}) fusion(f32[512,512]{1,0:T(8,128)S(1)} %copy-done.5), kind=kLoop, calls=%fused_computation.2 | loop fusion | bytes 3145728 | tf_op jit(solution)/shard_map/stack | solution.py:339
  39.8 4.2 %collective-permute-start.5 = (f32[2,128,512]{2,1,0:T(8,128)S(1)}, f32[2,128,512]{2,1,0:T(8,128)S(1)}, u32[]{:S(2)}, u32[]{:S(2)}) collective-permute-start(f32[2,128,512]{2,1,0:T(8,128)S(1)} %get-tuple-element.30), channel_id=1, source_target_pairs={{8,0},{16,8},{24,16},{9,1},{17,9},{25,17},{10,2},{18,10},{26,18},{... | collective-permute-start | bytes 1572872 | tf_op jit(solution)/shard_map/ppermute | solution.py:23
  45.6 4.8 %middle0.1.body = f32[2,768,512]{2,1,0:T(8,128)} custom-call(s32[3]{0:T(128)S(1)} %pad_add_fusion.cols_ref, f32[2,2,768,768]{3,2,1,0:T(8,128)} %tile.7, f32[2,2,768,128]{3,2,1,0:T(8,128)S(1)} %collective-permute-done.2.lt.lb.left, f32[2,2,768,128]{3,2,1,0:T(8,128)S(1)} %collective-permute-done.3.rt.rb.right), custom_call_target="tpu_custom_call" | custom-call | bytes 9437184 | tf_op jit(solution)/shard_map/middle0/pallas_call | solution.py:101
  50.4 4.9 %middle1.1.body = f32[2,768,512]{2,1,0:T(8,128)} custom-call(s32[3]{0:T(128)S(1)} %pad_add_fusion.cols_ref, f32[2,2,768,768]{3,2,1,0:T(8,128)} %tile.7, f32[2,2,768,128]{3,2,1,0:T(8,128)S(1)} %collective-permute-done.2.lt.lb.left, f32[2,2,768,128]{3,2,1,0:T(8,128)S(1)} %collective-permute-done.3.rt.rb.right), custom_call_target="tpu_custom_call" | custom-call | bytes 9437184 | tf_op jit(solution)/shard_map/middle1/pallas_call | solution.py:101
  55.4 11.3 %first.1.psi = f32[2,512,512]{2,1,0:T(8,128)S(1)} custom-call(s32[1]{0:T(128)} %bitcast.2.rows_ref, f32[2,128,512]{2,1,0:T(8,128)S(1)} %collective-permute-done.6.top, f32[2,768,512]{2,1,0:T(8,128)} %middle0.1.body, f32[2,128,512]{2,1,0:T(8,128)S(1)} %collective-permute-done.7.bottom, f32[2,512,512]{2,1,0:T(8,128)} %probe.3, ...), custom_call_target="tpu_custom_call" | custom-call | flops 4294967296 | bytes 12582912 | tf_op jit(solution)/shard_map/first/pallas_call | solution.py:358
  66.8 14.9 %second.1 = (f32[2,1032,512]{2,1,0:T(8,128)}, bf16[1024,512]{1,0:T(8,128)(2,1)S(1)}) custom-call(s32[1]{0:T(128)} %bitcast.2.rows_ref, s32[1]{0:T(128)} %bitcast.17.count_ref, f32[2,128,512]{2,1,0:T(8,128)S(1)} %collective-permute-done.4.top, f32[2,768,512]{2,1,0:T(8,128)} %middle1.1.body, f32[2,128,512]{2,1,0:T(8,128)S(1)} %collective-permute-done.5.bottom, ...), custom_call_target="tpu_custom_call" | custom-call | flops 4294967296 | bytes 14680064 | tf_op jit(solution)/shard_map/second/pallas_call | solution.py:367
  83.1 10.9 %collective-permute-start.13 = (f32[2,128,512]{2,1,0:T(8,128)S(1)}, f32[2,128,512]{2,1,0:T(8,128)S(1)}, u32[]{:S(2)}, u32[]{:S(2)}) collective-permute-start(f32[2,128,512]{2,1,0:T(8,128)S(1)} %get-tuple-element.23), channel_id=1, source_target_pairs={{8,0},{16,8},{24,16},{9,1},{17,9},{25,17},{10,2},{18,10},{26,18},{... | collective-permute-start | bytes 1572872 | tf_op jit(solution)/shard_map/ppermute | solution.py:23
  95.5 11.9 %third.1.grad = f32[2,1032,512]{2,1,0:T(8,128)} custom-call(s32[1]{0:T(128)} %bitcast.2.rows_ref, s32[1]{0:T(128)} %bitcast.18.count_ref, bf16[1024,512]{1,0:T(8,128)(2,1)S(1)} %get-tuple-element.15.back, f32[2,512,512]{2,1,0:T(8,128)S(1)} %copy-done.1, f32[2,512,512]{2,1,0:T(8,128)} %pad_maximum_fusion.k, bf16[512,512]{1,0:T(8,128)(2,1)S(1)} %copy-done.4, ...), custom_call_target="tpu_custom_call" | custom-call | flops 4294967296 | bytes 12582912 | tf_op jit(solution)/shard_map/third/pallas_call | solution.py:376
  108.7 5.6 %collective-permute-start.9 = (f32[2,128,512]{2,1,0:T(8,128)S(1)}, f32[2,128,512]{2,1,0:T(8,128)S(1)}, u32[]{:S(2)}, u32[]{:S(2)}) collective-permute-start(f32[2,128,512]{2,1,0:T(8,128)S(1)} %get-tuple-element.25), channel_id=1, source_target_pairs={{8,0},{16,8},{24,16},{9,1},{17,9},{25,17},{10,2},{18,10},{26,18},{... | collective-permute-start | bytes 1572872 | tf_op jit(solution)/shard_map/ppermute | solution.py:23
  115.7 2.4 %collective-permute-done.12.above = f32[2,128,512]{2,1,0:T(8,128)S(1)} collective-permute-done((f32[2,128,512]{2,1,0:T(8,128)S(1)}, f32[2,128,512]{2,1,0:T(8,128)S(1)}, u32[]{:S(2)}, u32[]{:S(2)}) %collective-permute-start.12) | collective-permute-done | bytes 524320 | tf_op jit(solution)/shard_map/ppermute | solution.py:23
  118.1 5.4 %spill1.1 = (f32[2,768,128]{2,1,0:T(8,128)S(1)}, f32[2,768,128]{2,1,0:T(8,128)S(1)}) custom-call(s32[3]{0:T(128)S(1)} %pad_add_fusion.cols_ref, f32[2,1032,512]{2,1,0:T(8,128)} %get-tuple-element.18.grad, f32[2,128,512]{2,1,0:T(8,128)S(1)} %collective-permute-done.12.above, f32[2,128,512]{2,1,0:T(8,128)S(1)} %collective-permute-done.13.below), custom_call_target="tpu_custom_call" | custom-call | bytes 7340032 | tf_op jit(solution)/shard_map/spill1/pallas_call | solution.py:305
  123.6 8.8 %collective-permute-start.14 = (f32[2,768,128]{2,1,0:T(8,128)S(1)}, f32[2,768,128]{2,1,0:T(8,128)S(1)}, u32[]{:S(2)}, u32[]{:S(2)}) collective-permute-start(f32[2,768,128]{2,1,0:T(8,128)S(1)} %get-tuple-element.19), channel_id=1, source_target_pairs={{0,1},{1,2},{2,3},{3,4},{4,5},{5,6},{6,7},{8,9},{9,10},{10,11},{11... | collective-permute-start | bytes 2359304 | tf_op jit(solution)/shard_map/ppermute | solution.py:23
  134.3 6.3 %collective-permute-done.8.above = f32[2,128,512]{2,1,0:T(8,128)S(1)} collective-permute-done((f32[2,128,512]{2,1,0:T(8,128)S(1)}, f32[2,128,512]{2,1,0:T(8,128)S(1)}, u32[]{:S(2)}, u32[]{:S(2)}) %collective-permute-start.8) | collective-permute-done | bytes 524320 | tf_op jit(solution)/shard_map/ppermute | solution.py:23
  140.6 5.4 %spill0.1 = (f32[2,768,128]{2,1,0:T(8,128)S(1)}, f32[2,768,128]{2,1,0:T(8,128)S(1)}) custom-call(s32[3]{0:T(128)S(1)} %pad_add_fusion.cols_ref, f32[2,1032,512]{2,1,0:T(8,128)} %third.1.grad, f32[2,128,512]{2,1,0:T(8,128)S(1)} %collective-permute-done.8.above, f32[2,128,512]{2,1,0:T(8,128)S(1)} %collective-permute-done.9.below), custom_call_target="tpu_custom_call" | custom-call | bytes 7340032 | tf_op jit(solution)/shard_map/spill0/pallas_call | solution.py:305
  146.0 6.2 %collective-permute-start.10 = (f32[2,768,128]{2,1,0:T(8,128)S(1)}, f32[2,768,128]{2,1,0:T(8,128)S(1)}, u32[]{:S(2)}, u32[]{:S(2)}) collective-permute-start(f32[2,768,128]{2,1,0:T(8,128)S(1)} %get-tuple-element.16), channel_id=1, source_target_pairs={{0,1},{1,2},{2,3},{3,4},{4,5},{5,6},{6,7},{8,9},{9,10},{10,11},{11... | collective-permute-start | bytes 2359304 | tf_op jit(solution)/shard_map/ppermute | solution.py:23
  154.2 8.3 %place1.1.rest_0_ = f32[2,2,768,768]{3,2,1,0:T(8,128)} custom-call(s32[3]{0:T(128)S(1)} %pad_add_fusion.cols_ref, f32[2]{0:T(128)S(1)} %copy-done, f32[2,1032,512]{2,1,0:T(8,128)} %get-tuple-element.18.grad, f32[2,128,512]{2,1,0:T(8,128)S(1)} %collective-permute-done.12.above, f32[2,128,512]{2,1,0:T(8,128)S(1)} %collective-permute-done.13.below, ...), custom_call_target="tpu_custom_call" | custom-call | bytes 14680064 | tf_op jit(solution)/shard_map/place1/pallas_call | solution.py:322
  162.5 3.0 %collective-permute-done.11.right = f32[2,768,128]{2,1,0:T(8,128)S(1)} collective-permute-done((f32[2,768,128]{2,1,0:T(8,128)S(1)}, f32[2,768,128]{2,1,0:T(8,128)S(1)}, u32[]{:S(2)}, u32[]{:S(2)}) %collective-permute-start.11) | collective-permute-done | bytes 786464 | tf_op jit(solution)/shard_map/ppermute | solution.py:23
  165.5 8.3 %place0.1 = f32[2,2,768,768]{3,2,1,0:T(8,128)} custom-call(s32[3]{0:T(128)S(1)} %pad_add_fusion.cols_ref, f32[2]{0:T(128)S(1)} %copy-done, f32[2,1032,512]{2,1,0:T(8,128)} %third.1.grad, f32[2,128,512]{2,1,0:T(8,128)S(1)} %collective-permute-done.8.above, f32[2,128,512]{2,1,0:T(8,128)S(1)} %collective-permute-done.9.below, ...), custom_call_target="tpu_custom_call", output_to_operand_aliasing={{}: (8, {})} | custom-call | bytes 14680064 | tf_op jit(solution)/shard_map/place0/pallas_call | solution.py:322
  (43 shorter events, 24.1 us)
Async XLA Ops:
  0.0 7.9 %copy-start.6 = (s32[1,1,1,2]{3,2,1,0:T(1,128)S(1)}, s32[1,1,1,2]{3,2,1,0:T(1,128)}, u32[]{:S(2)}) copy-start(s32[1,1,1,2]{3,2,1,0:T(1,128)} %param.13) | copy-start | bytes 28
  2.2 22.2 %collective-permute-start.3 = (f32[2,2,768,128]{3,2,1,0:T(8,128)S(1)}, f32[2,2,768,128]{3,2,1,0:T(8,128)S(1)}, u32[]{:S(2)}, u32[]{:S(2)}) collective-permute-start(f32[2,2,768,128]{3,2,1,0:T(8,128)S(1)} %get-tuple-element.21), channel_id=1, source_target_pairs={{1,0},{2,1},{3,2},{4,3},{5,4},{6,5},{7,6},{9,8},{10,9},{11,10},{12... | collective-permute-start | bytes 4718600 | tf_op jit(solution)/shard_map/ppermute | solution.py:23
  4.7 20.4 %collective-permute-start.2 = (f32[2,2,768,128]{3,2,1,0:T(8,128)S(1)}, f32[2,2,768,128]{3,2,1,0:T(8,128)S(1)}, u32[]{:S(2)}, u32[]{:S(2)}) collective-permute-start(f32[2,2,768,128]{3,2,1,0:T(8,128)S(1)} %get-tuple-element.22), channel_id=1, source_target_pairs={{0,1},{1,2},{2,3},{3,4},{4,5},{5,6},{6,7},{8,9},{9,10},{10,11},{11... | collective-permute-start | bytes 4718600 | tf_op jit(solution)/shard_map/ppermute | solution.py:23
  7.9 4.1 %collective-permute-start.1 = (s32[2]{0:T(128)S(1)}, s32[2]{0:T(128)S(1)}, u32[]{:S(2)}, u32[]{:S(2)}) collective-permute-start(s32[2]{0:T(128)S(1)} %bitcast.20), channel_id=1, source_target_pairs={{8,0},{16,8},{24,16},{9,1},{17,9},{25,17},{10,2},{18,10},{26,18},{... | collective-permute-start | bytes 32 | tf_op jit(solution)/shard_map/ppermute | solution.py:23
  10.0 4.6 %collective-permute-start = (s32[2]{0:T(128)S(1)}, s32[2]{0:T(128)S(1)}, u32[]{:S(2)}, u32[]{:S(2)}) collective-permute-start(s32[2]{0:T(128)S(1)} %bitcast.21), channel_id=1, source_target_pairs={{0,8},{8,16},{16,24},{1,9},{9,17},{17,25},{2,10},{10,18},{18,26},{... | collective-permute-start | bytes 32 | tf_op jit(solution)/shard_map/ppermute | solution.py:23
  28.5 6.3 %copy-start.5 = (f32[512,512]{1,0:T(8,128)S(1)}, f32[512,512]{1,0:T(8,128)}, u32[]{:S(2)}) copy-start(f32[512,512]{1,0:T(8,128)} %param.11) | copy-start | bytes 3145732
  28.6 26.8 %collective-permute-start.6 = (f32[2,128,512]{2,1,0:T(8,128)S(1)}, f32[2,128,512]{2,1,0:T(8,128)S(1)}, u32[]{:S(2)}, u32[]{:S(2)}) collective-permute-start(f32[2,128,512]{2,1,0:T(8,128)S(1)} %get-tuple-element.31), channel_id=1, source_target_pairs={{0,8},{8,16},{16,24},{1,9},{9,17},{17,25},{2,10},{10,18},{18,26},{... | collective-permute-start | bytes 1572872 | tf_op jit(solution)/shard_map/ppermute | solution.py:23
  30.1 25.3 %collective-permute-start.7 = (f32[2,128,512]{2,1,0:T(8,128)S(1)}, f32[2,128,512]{2,1,0:T(8,128)S(1)}, u32[]{:S(2)}, u32[]{:S(2)}) collective-permute-start(f32[2,128,512]{2,1,0:T(8,128)S(1)} %get-tuple-element.29), channel_id=1, source_target_pairs={{8,0},{16,8},{24,16},{9,1},{17,9},{25,17},{10,2},{18,10},{26,18},{... | collective-permute-start | bytes 1572872 | tf_op jit(solution)/shard_map/ppermute | solution.py:23
  38.5 28.3 %collective-permute-start.4 = (f32[2,128,512]{2,1,0:T(8,128)S(1)}, f32[2,128,512]{2,1,0:T(8,128)S(1)}, u32[]{:S(2)}, u32[]{:S(2)}) collective-permute-start(f32[2,128,512]{2,1,0:T(8,128)S(1)} %get-tuple-element.32), channel_id=1, source_target_pairs={{0,8},{8,16},{16,24},{1,9},{9,17},{17,25},{2,10},{10,18},{18,26},{... | collective-permute-start | bytes 1572872 | tf_op jit(solution)/shard_map/ppermute | solution.py:23
  39.8 27.0 %collective-permute-start.5 = (f32[2,128,512]{2,1,0:T(8,128)S(1)}, f32[2,128,512]{2,1,0:T(8,128)S(1)}, u32[]{:S(2)}, u32[]{:S(2)}) collective-permute-start(f32[2,128,512]{2,1,0:T(8,128)S(1)} %get-tuple-element.30), channel_id=1, source_target_pairs={{8,0},{16,8},{24,16},{9,1},{17,9},{25,17},{10,2},{18,10},{26,18},{... | collective-permute-start | bytes 1572872 | tf_op jit(solution)/shard_map/ppermute | solution.py:23
  50.4 5.0 %copy-start.3 = (bf16[512,512]{1,0:T(8,128)(2,1)S(1)}, bf16[512,512]{1,0:T(8,128)(2,1)}, u32[]{:S(2)}) copy-start(bf16[512,512]{1,0:T(8,128)(2,1)} %constant.5.clone.sin) | copy-start | bytes 1572868
  50.4 5.0 %copy-start.4 = (bf16[512,512]{1,0:T(8,128)(2,1)S(1)}, bf16[512,512]{1,0:T(8,128)(2,1)}, u32[]{:S(2)}) copy-start(bf16[512,512]{1,0:T(8,128)(2,1)} %constant.4.clone.cos) | copy-start | bytes 1572868
  55.4 11.4 %copy-start.2 = (bf16[1,1,1,512,512]{4,3,2,1,0:T(8,128)(2,1)S(1)}, bf16[1,1,1,512,512]{4,3,2,1,0:T(8,128)(2,1)}, u32[]{:S(2)}) copy-start(bf16[1,1,1,512,512]{4,3,2,1,0:T(8,128)(2,1)} %param.12) | copy-start | bytes 1572868
  81.7 13.9 %copy-start.1 = (f32[2,512,512]{2,1,0:T(8,128)S(1)}, f32[2,512,512]{2,1,0:T(8,128)}, u32[]{:S(2)}) copy-start(f32[2,512,512]{2,1,0:T(8,128)} %probe.3) | copy-start | bytes 6291460
  83.1 32.6 %collective-permute-start.13 = (f32[2,128,512]{2,1,0:T(8,128)S(1)}, f32[2,128,512]{2,1,0:T(8,128)S(1)}, u32[]{:S(2)}, u32[]{:S(2)}) collective-permute-start(f32[2,128,512]{2,1,0:T(8,128)S(1)} %get-tuple-element.23), channel_id=1, source_target_pairs={{8,0},{16,8},{24,16},{9,1},{17,9},{25,17},{10,2},{18,10},{26,18},{... | collective-permute-start | bytes 1572872 | tf_op jit(solution)/shard_map/ppermute | solution.py:23
  94.0 24.1 %collective-permute-start.12 = (f32[2,128,512]{2,1,0:T(8,128)S(1)}, f32[2,128,512]{2,1,0:T(8,128)S(1)}, u32[]{:S(2)}, u32[]{:S(2)}) collective-permute-start(f32[2,128,512]{2,1,0:T(8,128)S(1)} %get-tuple-element.24), channel_id=1, source_target_pairs={{0,8},{8,16},{16,24},{1,9},{9,17},{17,25},{2,10},{10,18},{18,26},{... | collective-permute-start | bytes 1572872 | tf_op jit(solution)/shard_map/ppermute | solution.py:23
  108.7 25.5 %collective-permute-start.9 = (f32[2,128,512]{2,1,0:T(8,128)S(1)}, f32[2,128,512]{2,1,0:T(8,128)S(1)}, u32[]{:S(2)}, u32[]{:S(2)}) collective-permute-start(f32[2,128,512]{2,1,0:T(8,128)S(1)} %get-tuple-element.25), channel_id=1, source_target_pairs={{8,0},{16,8},{24,16},{9,1},{17,9},{25,17},{10,2},{18,10},{26,18},{... | collective-permute-start | bytes 1572872 | tf_op jit(solution)/shard_map/ppermute | solution.py:23
  114.4 26.2 %collective-permute-start.8 = (f32[2,128,512]{2,1,0:T(8,128)S(1)}, f32[2,128,512]{2,1,0:T(8,128)S(1)}, u32[]{:S(2)}, u32[]{:S(2)}) collective-permute-start(f32[2,128,512]{2,1,0:T(8,128)S(1)} %get-tuple-element.26), channel_id=1, source_target_pairs={{0,8},{8,16},{16,24},{1,9},{9,17},{17,25},{2,10},{10,18},{18,26},{... | collective-permute-start | bytes 1572872 | tf_op jit(solution)/shard_map/ppermute | solution.py:23
  123.6 30.6 %collective-permute-start.14 = (f32[2,768,128]{2,1,0:T(8,128)S(1)}, f32[2,768,128]{2,1,0:T(8,128)S(1)}, u32[]{:S(2)}, u32[]{:S(2)}) collective-permute-start(f32[2,768,128]{2,1,0:T(8,128)S(1)} %get-tuple-element.19), channel_id=1, source_target_pairs={{0,1},{1,2},{2,3},{3,4},{4,5},{5,6},{6,7},{8,9},{9,10},{10,11},{11... | collective-permute-start | bytes 2359304 | tf_op jit(solution)/shard_map/ppermute | solution.py:23
  132.3 21.8 %copy-start = (f32[2]{0:T(128)S(1)}, f32[2]{0:T(128)}, u32[]{:S(2)}) copy-start(f32[2]{0:T(128)} %step_ref.3) | copy-start | bytes 28
  132.4 21.8 %collective-permute-start.15 = (f32[2,768,128]{2,1,0:T(8,128)S(1)}, f32[2,768,128]{2,1,0:T(8,128)S(1)}, u32[]{:S(2)}, u32[]{:S(2)}) collective-permute-start(f32[2,768,128]{2,1,0:T(8,128)S(1)} %get-tuple-element.20), channel_id=1, source_target_pairs={{1,0},{2,1},{3,2},{4,3},{5,4},{6,5},{7,6},{9,8},{10,9},{11,10},{12... | collective-permute-start | bytes 2359304 | tf_op jit(solution)/shard_map/ppermute | solution.py:23
  146.0 16.5 %collective-permute-start.10 = (f32[2,768,128]{2,1,0:T(8,128)S(1)}, f32[2,768,128]{2,1,0:T(8,128)S(1)}, u32[]{:S(2)}, u32[]{:S(2)}) collective-permute-start(f32[2,768,128]{2,1,0:T(8,128)S(1)} %get-tuple-element.16), channel_id=1, source_target_pairs={{0,1},{1,2},{2,3},{3,4},{4,5},{5,6},{6,7},{8,9},{9,10},{10,11},{11... | collective-permute-start | bytes 2359304 | tf_op jit(solution)/shard_map/ppermute | solution.py:23
  152.2 13.3 %collective-permute-start.11 = (f32[2,768,128]{2,1,0:T(8,128)S(1)}, f32[2,768,128]{2,1,0:T(8,128)S(1)}, u32[]{:S(2)}, u32[]{:S(2)}) collective-permute-start(f32[2,768,128]{2,1,0:T(8,128)S(1)} %get-tuple-element.17), channel_id=1, source_target_pairs={{1,0},{2,1},{3,2},{4,3},{5,4},{6,5},{7,6},{9,8},{10,9},{11,10},{12... | collective-permute-start | bytes 2359304 | tf_op jit(solution)/shard_map/ppermute | solution.py:23
